TPU v7x, 256 devices: a whole 4x4x8 slice. The times are simulated.
256 devices in a mesh: grp: 2 (over x_lo), ty: 4 (over x_hi, core), tx: 32 (over y, z).
Axes of the slice: x: 4 (x_hi: 2, x_lo: 2; x = x_hi * 2 + x_lo), y: 4, z: 8, core: 2. Of those that a mesh axis runs over, the one named last changes fastest.
Arguments:
- adjoint_state: float32 [2, 5, 50, 384, 1536], P('grp', None, None, 'tx', 'ty'), may hold values from -6 to 6
- land_mask: int32 [2, 384, 1536], P('grp', 'tx', 'ty'), may hold values 0 or 1
- diffusivity: float32 [2, 384, 1536], P('grp', 'tx', 'ty'), may hold values from 0.02 to 0.24
- mixing: float32 [2, 5, 50, 50], P('grp'), may hold values from -0.875 to 0.875
- nudging: float32 [384, 1536], P('tx', 'ty'), may hold values from 0.1 to 1
- nest_x: int32 [128], P(('ty', 'tx')), may hold values from 0 to 8
- nest_y: int32 [128], P(('ty', 'tx')), may hold values from 0 to 256
- obs_forcing: float32 [2, 128, 16, 128], P('grp', ('ty', 'tx')), may hold values from -6 to 6
- obs_cell: int32 [2, 128, 16, 128], P('grp', None, None, ('ty', 'tx')), may hold values from 0 to 1151999
- obs_count: int32 [2, 128, 128], P('grp', None, ('ty', 'tx')), may hold values from 0 to 16, as said below
Outputs:
- updated_state: float32 [2, 5, 50, 384, 1536], P('grp', None, None, 'tx', 'ty')
Inputs may be any that keep to these rules, and one draw needn't show every extreme that they name: `obs_count`: in every draw some destination tile of each grid receives 16 live slots from every source tile; which one is drawn.
All inputs are finite; a program needn't handle non-finite values. No bound on the sum of `land_mask` on one device may be relied on, other than what follows from the above.
Results may differ from a plain program's by a relative error of at most 0.0003.
Values sent between devices are 32-bit elements; how exact they have to be, the bound alone decides.
A program may use at most 128 MiB of HBM per device.

v0:
```python
import jax
import jax.numpy as jnp
from jax import lax
from jax.sharding import PartitionSpec as P


def with_halo(cells, sides, width):
    for axis, dim in sides:
        count = lax.axis_size(axis)
        ends = count - 1
        head = lax.slice_in_dim(cells, 0, width, axis=dim)
        tail = lax.slice_in_dim(cells, cells.shape[dim] - width, cells.shape[dim], axis=dim)
        cells = jnp.concatenate(
            [
                lax.ppermute(tail, axis, [(i, (i + 1) % count) for i in range(ends)]),
                cells,
                lax.ppermute(head, axis, [((i + 1) % count, i) for i in range(ends)]),
            ],
            axis=dim,
        )
    return cells


def swapped(value, axis, stride):
    mask = 2**stride
    pairs = [(source, source ^ mask) for source in range(lax.axis_size(axis))]
    return lax.ppermute(value, axis, pairs)


def local(
    adjoint_state,
    land_mask,
    diffusivity,
    mixing,
    nudging,
    nest_x,
    nest_y,
    obs_forcing,
    obs_cell,
    obs_count,
):
    state = adjoint_state[0]
    fields, levels, cols, rows = state.shape
    mask = land_mask[0].astype(jnp.float32)
    kappa = diffusivity[0]
    masked = state * mask[None, None]
    padded = with_halo(masked, (("ty", 3), ("tx", 2)), 1)
    beside_all = padded[:, :, 2:, 1:-1] + padded[:, :, :-2, 1:-1]
    beside_all = beside_all + padded[:, :, 1:-1, 2:] + padded[:, :, 1:-1, :-2]
    field = masked + kappa * (beside_all - 4.0 * masked)
    flat = field.reshape(fields, levels, cols * rows)
    mixed = jnp.einsum("fkl,flc->fkc", mixing[0], flat, precision=lax.Precision.HIGHEST).reshape(
        field.shape
    )
    third_x = cols // 3
    third_y = rows // 3
    reduced = (nudging * mixed).reshape(fields, levels, third_x, 3, third_y, 3).sum(axis=(3, 5))
    start = (jnp.int32(0), jnp.int32(0), nest_x[0], nest_y[0])
    block = lax.dynamic_slice(mixed, start, (fields, levels, third_x, third_y))
    is_child = lax.axis_index("grp") == 0
    payload = jnp.where(is_child, reduced, block)
    partner = swapped(payload, "grp", 0)
    slots = obs_forcing.shape[2]
    arrived = lax.all_to_all(
        obs_forcing, ("ty", "tx"), split_axis=3, concat_axis=1, tiled=True
    ).reshape(-1, slots)
    sources = arrived.shape[0]
    live = lax.broadcasted_iota(jnp.int32, (sources, slots), 1) < obs_count[0]
    cells = obs_cell[0, :, :, 0].reshape(-1)
    added = jnp.where(live, arrived, jnp.zeros_like(arrived)).reshape(-1)
    forced = mixed.reshape(-1).at[cells].add(added).reshape(mixed.shape)
    col_ids = lax.broadcasted_iota(jnp.int32, (cols, third_x), 0)
    col_sub = lax.broadcasted_iota(jnp.int32, (cols, third_x), 1)
    row_ids = lax.broadcasted_iota(jnp.int32, (rows, third_y), 0)
    row_sub = lax.broadcasted_iota(jnp.int32, (rows, third_y), 1)
    place_x = jnp.where(is_child, col_ids // 3 == col_sub, col_ids == nest_x[0] + col_sub).astype(
        jnp.float32
    )
    place_y = jnp.where(is_child, row_ids // 3 == row_sub, row_ids == nest_y[0] + row_sub).astype(
        jnp.float32
    )
    delta = jnp.where(is_child, partner / 9.0, partner - block)
    along_y = jnp.einsum("flij,yj->fliy", delta, place_y, precision=lax.Precision.HIGHEST)
    correction = jnp.einsum("xi,fliy->flxy", place_x, along_y, precision=lax.Precision.HIGHEST)
    result = forced + correction
    return (result * mask[None, None])[None]


def solution(mesh):
    in_specs = (
        P("grp", None, None, "tx", "ty"),
        P("grp", "tx", "ty"),
        P("grp", "tx", "ty"),
        P("grp", None, None, None),
        P("tx", "ty"),
        P(("ty", "tx")),
        P(("ty", "tx")),
        P("grp", ("ty", "tx"), None, None),
        P("grp", None, None, ("ty", "tx")),
        P("grp", None, ("ty", "tx")),
    )
    out_specs = P("grp", None, None, "tx", "ty")
    return jax.shard_map(local, mesh=mesh, in_specs=in_specs, out_specs=out_specs, check_vma=False)
```

profile of v0, /device:TPU:25, one launch (start us, length us, event | category | flops | bytes accessed | tf_op | source)
XLA Modules:
  0.0 189.7 jit_solution(18040988435356274102)
XLA Ops:
  0.8 2.9 %bitcast_multiply_fusion = f32[5,50,12,384]{3,2,1,0:T(8,128)S(1)} fusion(f32[1,5,50,12,384]{4,0,3,2,1:T(1,128)} %param.10, f32[12,384]{1,0:T(8,128)S(1)} %bitcast.64), kind=kLoop, calls=%fused_computation.20 | loop fusion | flops 1152000 | bytes 9234432 | tf_op jit(solution)/shard_map/mul | solution.py:46
  3.7 2.6 %copy-done = f32[5,50,12,384]{3,2,1,0:T(8,128)} copy-done((f32[5,50,12,384]{3,2,1,0:T(8,128)}, f32[5,50,12,384]{3,2,1,0:T(8,128)S(1)}, u32[]{:S(2)}) %copy-start) | copy-done | bytes 4608024
  8.3 2.3 %copy.35 = f32[5,50,12,1]{1,3,2,0:T(1,128)S(1)} copy(f32[5,50,12,1]{3,2,1,0:T(8,128)} %get-tuple-element.8) | data formatting | bytes 24000 | tf_op jit(solution)/shard_map/slice | solution.py:12
  10.5 5.2 %collective-permute-start = (f32[5,50,12,1]{1,3,2,0:T(1,128)S(1)}, f32[5,50,12,1]{1,3,2,0:T(1,128)S(1)}, u32[]{:S(2)}, u32[]{:S(2)}) collective-permute-start(f32[5,50,12,1]{1,3,2,0:T(1,128)S(1)} %copy.35), channel_id=1, source_target_pairs={{0,32},{32,64},{64,96},{1,33},{33,65},{65,97},{2,34},{34,66},{66,9... | collective-permute-start | bytes 36008 | tf_op jit(solution)/shard_map/ppermute | solution.py:15
  19.1 15.6 %all-to-all-start = ((f32[1,1,16,128]{2,1,0,3:T(1,128)}), f32[1,1,16,128]{2,1,0,3:T(1,128)S(1)}, u32[]{:S(2)}, u32[]{:S(2)}) async-start(f32[1,1,16,128]{2,1,0,3:T(1,128)} %copy.42), calls=%async_computation | async-start | bytes 131072 | tf_op jit(solution)/shard_map/all_to_all | solution.py:64
  37.0 2.2 %copy.37 = f32[5,50,12,1]{3,2,1,0:T(8,128)} copy(f32[5,50,12,1]{1,3,2,0:T(1,128)S(1)} %collective-permute-done) | data formatting | bytes 24000 | tf_op jit(solution)/shard_map/ppermute | solution.py:15
  39.2 2.2 %copy.38 = f32[5,50,12,1]{3,2,1,0:T(8,128)} copy(f32[5,50,12,1]{1,3,2,0:T(1,128)S(1)} %collective-permute-done.1) | data formatting | bytes 24000 | tf_op jit(solution)/shard_map/ppermute | solution.py:17
  41.4 6.3 %pad_maximum_fusion.10 = (f32[5,50,1,386]{3,2,1,0:T(1,128)S(1)}, f32[5,50,1,386]{3,2,1,0:T(1,128)S(1)}) fusion(f32[5,50,12,1]{3,2,1,0:T(8,128)} %copy.38, f32[5,50,12,384]{3,2,1,0:T(8,128)} %copy-done, f32[5,50,12,1]{3,2,1,0:T(8,128)} %copy.37), kind=kLoop, calls=%fused_computation.32 | loop fusion | flops 386000 | bytes 5404000 | tf_op jit(solution)/shard_map/slice | solution.py:11
  47.7 4.6 %collective-permute-start.2 = (f32[5,50,1,386]{3,2,1,0:T(1,128)S(1)}, f32[5,50,1,386]{3,2,1,0:T(1,128)S(1)}, u32[]{:S(2)}, u32[]{:S(2)}) collective-permute-start(f32[5,50,1,386]{3,2,1,0:T(1,128)S(1)} %get-tuple-element.5), channel_id=1, source_target_pairs={{1,0},{2,1},{3,2},{4,3},{5,4},{6,5},{7,6},{8,7},{9,8},{10,9},{11,1... | collective-permute-start | bytes 1158008 | tf_op jit(solution)/shard_map/ppermute | solution.py:17
  52.3 2.1 %collective-permute-start.3 = (f32[5,50,1,386]{3,2,1,0:T(1,128)S(1)}, f32[5,50,1,386]{3,2,1,0:T(1,128)S(1)}, u32[]{:S(2)}, u32[]{:S(2)}) collective-permute-start(f32[5,50,1,386]{3,2,1,0:T(1,128)S(1)} %get-tuple-element.6), channel_id=1, source_target_pairs={{0,1},{1,2},{2,3},{3,4},{4,5},{5,6},{6,7},{7,8},{8,9},{9,10},{10,1... | collective-permute-start | bytes 1158008 | tf_op jit(solution)/shard_map/ppermute | solution.py:15
  54.5 8.7 %collective-permute-done.2 = f32[5,50,1,386]{3,2,1,0:T(1,128)S(1)} collective-permute-done((f32[5,50,1,386]{3,2,1,0:T(1,128)S(1)}, f32[5,50,1,386]{3,2,1,0:T(1,128)S(1)}, u32[]{:S(2)}, u32[]{:S(2)}) %collective-permute-start.2) | collective-permute-done | bytes 386032 | tf_op jit(solution)/shard_map/ppermute | solution.py:17
  63.2 5.9 %collective-permute-done.3 = f32[5,50,1,386]{3,2,1,0:T(1,128)S(1)} collective-permute-done((f32[5,50,1,386]{3,2,1,0:T(1,128)S(1)}, f32[5,50,1,386]{3,2,1,0:T(1,128)S(1)}, u32[]{:S(2)}, u32[]{:S(2)}) %collective-permute-start.3) | collective-permute-done | bytes 386032 | tf_op jit(solution)/shard_map/ppermute | solution.py:15
  69.1 9.9 %fusion.3 = f32[5,50,12,384]{3,2,1,0:T(8,128)} fusion(f32[5,50,12,384]{3,2,1,0:T(8,128)S(1)} %bitcast.60, f32[5,50,12,1]{3,2,1,0:T(8,128)S(1)} %copy-done.1, f32[5,50,12,1]{3,2,1,0:T(8,128)S(1)} %copy-done.2, f32[5,50,1,386]{3,2,1,0:T(1,128)S(1)} %collective-permute-done.3, f32[5,50,1,386]{3,2,1,0:T(1,128)S(1)} %collective-permute-done.2, ...), kind=kLoop, calls=%fused_computation.7 | loop fusion | flops 17280000 | bytes 10030432 | tf_op jit(solution)/shard_map/add | solution.py:50
  79.1 6.9 %reshape.61 = f32[5,50,4608]{2,1,0:T(8,128)} reshape(f32[5,50,12,384]{3,2,1,0:T(8,128)} %fusion.3) | data formatting | bytes 9216000 | tf_op jit(solution)/shard_map/reshape | solution.py:51
  86.0 9.3 %convolution_bitcast_fusion = f32[5,50,4608]{2,1,0:T(8,128)} fusion(f32[5,50,4608]{2,1,0:T(8,128)} %reshape.61, f32[1,5,50,50]{3,0,2,1:T(1,128)S(1)} %copy-done.3), kind=kOutput, calls=%fused_computation.2 | convolution fusion | flops 691200000 | bytes 9266000 | tf_op jit(solution)/shard_map/fkl,flc->fkc/dot_general | solution.py:52
  95.3 9.2 %copy.43 = f32[5,50,4608]{1,2,0:T(8,128)} copy(f32[5,50,4608]{2,1,0:T(8,128)} %convolution_bitcast_fusion) | data formatting | bytes 9216000 | tf_op jit(solution)/shard_map/fkl,flc->fkc/dot_general | solution.py:52
  104.5 18.4 %reshape.64 = f32[5,50,4,3,128,3]{1,5,4,3,2,0:T(4,128)} reshape(f32[5,50,4608]{1,2,0:T(8,128)} %copy.43) | data formatting | bytes 9216000 | tf_op jit(solution)/shard_map/reshape | solution.py:52
  122.9 15.7 %multiply_reduce_fusion = f32[5,50,4,128]{1,3,2,0:T(8,128)S(1)} fusion(f32[5,50,4,3,128,3]{1,5,4,3,2,0:T(4,128)} %reshape.64, f32[4,3,128,3]{3,2,1,0:T(8,128)S(1)} %mul.48), kind=kLoop, calls=%fused_computation.1 | loop fusion | flops 2176000 | bytes 5138432 | tf_op jit(solution)/shard_map/reduce_sum | solution.py:57
  141.3 4.9 %reshape_reshape.3 = f32[1152000]{0:T(1024)} reshape(f32[5,50,4608]{2,1,0:T(8,128)} %convolution_bitcast_fusion) | data formatting | bytes 9216000 | tf_op jit(solution)/shard_map/reshape;reshape | solution.py:71
  146.2 14.8 %scatter_fusion = f32[1152000]{0:T(1024)} fusion(f32[1152000]{0:T(1024)} %reshape_reshape.3, s32[2048]{0:T(1024)S(1)} %bitcast.67, f32[2048]{0:T(1024)S(1)} %broadcast_select_fusion), kind=kCustom, calls=%fused_computation | custom fusion | flops 2048 | bytes 32768 | tf_op jit(solution)/shard_map/scatter-add | solution.py:71
  160.9 6.7 %reshape.63 = f32[5,50,12,384]{3,2,1,0:T(8,128)} reshape(f32[1152000]{0:T(1024)} %scatter_fusion) | data formatting | bytes 9216000 | tf_op jit(solution)/shard_map/reshape | solution.py:71
  168.0 3.7 %fusion.9 = f32[5,50,4,384]{3,1,2,0:T(8,128)S(1)} fusion(f32[5,50,4,128]{1,3,2,0:T(8,128)S(1)} %copy.46, f32[5,50,12,384]{1,3,2,0:T(8,128)} %bitcast.62, s32[]{:T(128)S(6)} %select_n.62, s32[]{:T(128)S(6)} %select_n.63, pred[]{:T(512)S(6)} %eq.15, s32[128]{0:T(128)S(1)} %iota_add_fusion.1, s32[384]{0:T(512)S(1)} %get-tuple-element.9, ...), kind=kOutput, calls=%fused_computation.22 | convolution fusion | flops 590404608 | bytes 3364736 | tf_op jit(solution)/shard_map/flij,yj->fliy/dot_general | solution.py:83
  171.8 8.3 %fusion.7 = f32[1,5,50,12,384]{4,3,2,1,0:T(8,128)} fusion(f32[5,50,12,384]{3,2,1,0:T(8,128)} %reshape.63, f32[12,384]{1,0:T(8,128)S(1)} %bitcast.65, f32[5,50,4,384]{3,1,2,0:T(8,128)S(1)} %fusion.9, s32[4]{0:T(128)S(1)} %iota_add_fusion, s32[12]{0:T(128)S(1)} %get-tuple-element.11, s32[12]{0:T(128)S(1)} %get-tuple-element.12, ...), kind=kOutput, calls=%fused_computation.19 | convolution fusion | flops 57600192 | bytes 10770557 | tf_op jit(solution)/shard_map/xi,fliy->flxy/dot_general | solution.py:84
  180.1 9.6 %copy.50 = f32[1,5,50,12,384]{4,0,3,2,1:T(1,128)} copy(f32[1,5,50,12,384]{4,3,2,1,0:T(8,128)} %fusion.7) | data formatting | bytes 9216000 | tf_op jit(solution)/shard_map/broadcast_in_dim | solution.py:86
  (51 shorter events, 10.1 us)
Async XLA Ops:
  3.7 2.6 %copy-start = (f32[5,50,12,384]{3,2,1,0:T(8,128)}, f32[5,50,12,384]{3,2,1,0:T(8,128)S(1)}, u32[]{:S(2)}) copy-start(f32[5,50,12,384]{3,2,1,0:T(8,128)S(1)} %bitcast_multiply_fusion) | copy-start | bytes 13824004
  6.3 12.1 %copy-start.6 = (f32[1,1,16,128]{3,2,1,0:T(8,128)S(1)}, f32[1,1,16,128]{3,2,1,0:T(8,128)}, u32[]{:S(2)}) copy-start(f32[1,1,16,128]{3,2,1,0:T(8,128)} %param.17) | copy-start | bytes 24580
  6.3 29.2 %copy-start.5 = (f32[1,12,384]{2,0,1:T(1,128)S(1)}, f32[1,12,384]{2,0,1:T(1,128)}, u32[]{:S(2)}) copy-start(f32[1,12,384]{2,0,1:T(1,128)} %param.12) | copy-start | bytes 55300
  6.3 29.2 %copy-start.4 = (f32[12,384]{1,0:T(8,128)S(1)}, f32[12,384]{1,0:T(8,128)}, u32[]{:S(2)}) copy-start(f32[12,384]{1,0:T(8,128)} %param.14) | copy-start | bytes 55300
  6.3 30.5 %copy-start.7 = (s32[1,128,16,1]{1,3,2,0:T(1,128)S(1)}, s32[1,128,16,1]{1,3,2,0:T(1,128)}, u32[]{:S(2)}) copy-start(s32[1,128,16,1]{1,3,2,0:T(1,128)} %param.18) | copy-start | bytes 24580
  10.5 26.4 %collective-permute-start = (f32[5,50,12,1]{1,3,2,0:T(1,128)S(1)}, f32[5,50,12,1]{1,3,2,0:T(1,128)S(1)}, u32[]{:S(2)}, u32[]{:S(2)}) collective-permute-start(f32[5,50,12,1]{1,3,2,0:T(1,128)S(1)} %copy.35), channel_id=1, source_target_pairs={{0,32},{32,64},{64,96},{1,33},{33,65},{65,97},{2,34},{34,66},{66,9... | collective-permute-start | bytes 36008 | tf_op jit(solution)/shard_map/ppermute | solution.py:15
  16.5 22.7 %collective-permute-start.1 = (f32[5,50,12,1]{1,3,2,0:T(1,128)S(1)}, f32[5,50,12,1]{1,3,2,0:T(1,128)S(1)}, u32[]{:S(2)}, u32[]{:S(2)}) collective-permute-start(f32[5,50,12,1]{1,3,2,0:T(1,128)S(1)} %copy.36), channel_id=1, source_target_pairs={{32,0},{64,32},{96,64},{33,1},{65,33},{97,65},{34,2},{66,34},{98,6... | collective-permute-start | bytes 36008 | tf_op jit(solution)/shard_map/ppermute | solution.py:17
  19.1 122.1 %all-to-all-start = ((f32[1,1,16,128]{2,1,0,3:T(1,128)}), f32[1,1,16,128]{2,1,0,3:T(1,128)S(1)}, u32[]{:S(2)}, u32[]{:S(2)}) async-start(f32[1,1,16,128]{2,1,0,3:T(1,128)} %copy.42), calls=%async_computation | async-start | bytes 131072 | tf_op jit(solution)/shard_map/all_to_all | solution.py:64
  39.2 29.9 %slice-start = ((s8[6144000]{0:T(1024)(128)(4,1)}), s8[1949696]{0:T(1024)(128)(4,1)S(1)}, s32[]{:S(2)}) async-start(s8[6144000]{0:T(1024)(128)(4,1)} %bitcast.59), calls=%async_computation.1 | async-start | bytes 3899392
  41.4 27.7 %slice-start.1 = ((s8[6144000]{0:T(1024)(128)(4,1)}), s8[4194304]{0:T(1024)(128)(4,1)S(1)}, s32[]{:S(2)}) async-start(s8[6144000]{0:T(1024)(128)(4,1)} %bitcast.59), calls=%async_computation.2 | async-start | bytes 8388608
  41.4 27.7 %copy-start.1 = (f32[5,50,12,1]{3,2,1,0:T(8,128)S(1)}, f32[5,50,12,1]{3,2,1,0:T(8,128)}, u32[]{:S(2)}) copy-start(f32[5,50,12,1]{3,2,1,0:T(8,128)} %copy.37) | copy-start | bytes 36004
  41.4 27.7 %copy-start.2 = (f32[5,50,12,1]{3,2,1,0:T(8,128)S(1)}, f32[5,50,12,1]{3,2,1,0:T(8,128)}, u32[]{:S(2)}) copy-start(f32[5,50,12,1]{3,2,1,0:T(8,128)} %copy.38) | copy-start | bytes 36004
  47.7 15.5 %collective-permute-start.2 = (f32[5,50,1,386]{3,2,1,0:T(1,128)S(1)}, f32[5,50,1,386]{3,2,1,0:T(1,128)S(1)}, u32[]{:S(2)}, u32[]{:S(2)}) collective-permute-start(f32[5,50,1,386]{3,2,1,0:T(1,128)S(1)} %get-tuple-element.5), channel_id=1, source_target_pairs={{1,0},{2,1},{3,2},{4,3},{5,4},{6,5},{7,6},{8,7},{9,8},{10,9},{11,1... | collective-permute-start | bytes 1158008 | tf_op jit(solution)/shard_map/ppermute | solution.py:17
  52.3 16.8 %collective-permute-start.3 = (f32[5,50,1,386]{3,2,1,0:T(1,128)S(1)}, f32[5,50,1,386]{3,2,1,0:T(1,128)S(1)}, u32[]{:S(2)}, u32[]{:S(2)}) collective-permute-start(f32[5,50,1,386]{3,2,1,0:T(1,128)S(1)} %get-tuple-element.6), channel_id=1, source_target_pairs={{0,1},{1,2},{2,3},{3,4},{4,5},{5,6},{6,7},{7,8},{8,9},{9,10},{10,1... | collective-permute-start | bytes 1158008 | tf_op jit(solution)/shard_map/ppermute | solution.py:15
  79.1 6.9 %copy-start.3 = (f32[1,5,50,50]{3,0,2,1:T(1,128)S(1)}, f32[1,5,50,50]{3,0,2,1:T(1,128)}, u32[]{:S(2)}) copy-start(f32[1,5,50,50]{3,0,2,1:T(1,128)} %param.13) | copy-start | bytes 150004
  122.9 18.1 %copy-start.8 = (s32[1,128,1]{1,2,0:T(1,128)S(1)}, s32[1,128,1]{1,2,0:T(1,128)}, u32[]{:S(2)}) copy-start(s32[1,128,1]{1,2,0:T(1,128)} %param.19) | copy-start | bytes 1540
  140.6 27.0 %collective-permute-start.4 = (f32[5,50,4,128]{3,2,1,0:T(4,128)S(1)}, f32[5,50,4,128]{3,2,1,0:T(4,128)S(1)}, u32[]{:S(2)}, u32[]{:S(2)}) collective-permute-start(f32[5,50,4,128]{3,2,1,0:T(4,128)S(1)} %copy.45), channel_id=1, source_target_pairs={{0,128},{128,0},{1,129},{129,1},{2,130},{130,2},{3,131},{131,3},{4... | collective-permute-start | bytes 1536008 | tf_op jit(solution)/shard_map/ppermute | solution.py:27
where the time goes:
time: 193 us; the launch traced here: 190 us
  local copies, waits for them, and re-layouts  70.3 us (36%)
  other arithmetic  52 us (27%)
  starting transfers between devices  29.8 us (15%)
  matrix products  21.4 us (11%)
  waiting for transfers between devices  14.7 us (8%)
    reshape x1, local copies, waits for them, and re-layouts, local(): jnp.einsum('fkl,flc->fkc', mixing[0], flat, precision=lax.Precision.HIGHEST)  18.4 us
    reduce_sum x1, other arithmetic, local(): (nudging * mixed).reshape(fields, levels, third_x, 3, third_y, 3)  15.7 us
    all_to_all x1, starting transfers between devices, local(): lax.all_to_all(obs_forcing, ('ty', 'tx'), split_axis=3, concat_axis=1, ti...  15.6 us
    scatter-add x1, other arithmetic, local(): forced = mixed.reshape(-1).at[cells].add(added).reshape(mixed.shape)  14.8 us
    add x1, other arithmetic, local(): field = masked + kappa * (beside_all - 4.0 * masked)  9.93 us
    broadcast_in_dim x1, local copies, waits for them, and re-layouts, local(): return (result * mask[None, None])[None]  9.63 us
    dot_general x1, matrix products, local(): jnp.einsum('fkl,flc->fkc', mixing[0], flat, precision=lax.Precision.HIGHEST)  9.33 us
    dot_general x1, local copies, waits for them, and re-layouts, local(): jnp.einsum('fkl,flc->fkc', mixing[0], flat, precision=lax.Precision.HIGHEST)  9.18 us
  transfers between devices with their start and end apart: 6, of which 2 were waited for; matrix products, arithmetic and copies ran while one was open for 59% of the time, Pallas kernels for 0%

commit v1 on v0

v1 whole, which is shorter than its diff:
```python
import functools

import jax
import jax.numpy as jnp
from jax import lax
from jax.experimental import pallas as pl
from jax.experimental.pallas import tpu as pltpu
from jax.sharding import PartitionSpec as P

MESH = pl.DeviceIdType.MESH
F32 = jnp.float32
BF16 = jnp.bfloat16
NF, NL, NXC, NYC = 5, 50, 12, 384
LP = 56
NB = NYC // 128
ROWS = NL * NXC * NB
STEP = NXC * NB
NTY, NTX, NYA, NZA = 4, 32, 4, 8
SLOTS = 16


def split(value):
    high = value.astype(BF16)
    low = (value - high.astype(F32)).astype(BF16)
    return high, low


def exchange_kernel(
    nest_x, nest_y, state, mask, kappa, nudge, mix, obs,
    out, obs_out,
    raw, ms, xs, mc, mx, wsel, wback, lhs, pay, got, dlt, cu,
    ycols, yhalo, oa, ob, oc, od, oe, og,
    in_sem, hs_sem, hr_sem, ys_sem, yr_sem, gs_sem, gr_sem,
    os1, or1, os2, or2, os3, or3,
):
    grp = lax.axis_index("grp")
    ty = lax.axis_index("ty")
    tx = lax.axis_index("tx")
    ya, za = tx // NZA, tx % NZA
    child = grp == 0
    parent = grp == 1

    def dev(g=None, y=None, x=None):
        return (grp if g is None else g, ty if y is None else y, tx if x is None else x)

    def fetch(f):
        return pltpu.make_async_copy(state.at[f], raw.at[f], in_sem.at[f])

    for f in range(NF):
        fetch(f).start()

    barrier = pltpu.get_barrier_semaphore()

    def greet(target):
        pl.semaphore_signal(barrier, inc=1, device_id=target, device_id_type=MESH)

    has_left, has_right = tx > 0, tx < NTX - 1
    has_down, has_up = ty > 0, ty < NTY - 1
    greet(dev(g=1 - grp))
    for d in range(1, NTY):
        greet(dev(y=(ty + d) % NTY))
    for d in range(1, NYA):
        greet(dev(x=((ya + d) % NYA) * NZA + za))
    for d in range(1, NZA):
        greet(dev(x=ya * NZA + (za + d) % NZA))

    @pl.when(has_left)
    def _():
        greet(dev(x=tx - 1))

    @pl.when(has_right)
    def _():
        greet(dev(x=tx + 1))

    oa[:, 0:SLOTS] = obs[...].T
    lane = lax.broadcasted_iota(jnp.int32, (NL, 128), 1)
    scale = jnp.where(child, 3, 1)
    off = jnp.where(child, 0, nest_y[0])

    def selection(shape, ydim):
        d = lax.broadcasted_iota(jnp.int32, shape, ydim)
        d = d - scale * lax.broadcasted_iota(jnp.int32, shape, 1 - ydim) - off
        return jnp.where((d >= 0) & (d < scale), 1.0, 0.0).astype(BF16)

    wsel[...] = selection((NYC, 128), 0)
    wback[...] = selection((128, NYC), 1)
    mc[...] = jnp.zeros_like(mc)
    xs[...] = jnp.zeros_like(xs)
    for f in range(NF):
        high, low = split(mix[f])
        mc[f, 0:NL, 0:NL] = high
        mc[f, 0:NL, 64:64 + NL] = high
        mc[f, 0:NL, 128:128 + NL] = low
    cu[4] = jnp.zeros(cu.shape[1:], F32)
    ycols[...] = jnp.zeros_like(ycols)

    @pl.when(tx == 0)
    def _():
        for f in range(NF):
            ms[f, 0] = jnp.zeros(ms.shape[2:], F32)

    @pl.when(tx == NTX - 1)
    def _():
        for f in range(NF):
            ms[f, NXC + 1] = jnp.zeros(ms.shape[2:], F32)

    @pl.when(ty == 0)
    def _():
        yhalo[0] = jnp.zeros(yhalo.shape[1:], F32)

    @pl.when(ty == NTY - 1)
    def _():
        yhalo[1] = jnp.zeros(yhalo.shape[1:], F32)

    pl.semaphore_wait(
        barrier,
        1 + (NTY - 1) + (NYA - 1) + (NZA - 1) + jnp.where(has_left, 1, 0) + jnp.where(has_right, 1, 0),
    )

    def obs1(d):
        peer = (ty + d) % NTY
        return pltpu.make_async_remote_copy(
            oa.at[pl.ds(pl.multiple_of(peer * NTX, NTX), NTX)], ob.at[ty], os1.at[d - 1], or1.at[d - 1],
            device_id=dev(y=peer), device_id_type=MESH,
        )

    def obs2(d):
        peer = (ya + d) % NYA
        return pltpu.make_async_remote_copy(
            oc.at[pl.ds(pl.multiple_of(peer * NZA, NZA), NZA)],
            od.at[pl.ds(pl.multiple_of(ya * NZA, NZA), NZA)], os2.at[d - 1], or2.at[d - 1],
            device_id=dev(x=peer * NZA + za), device_id_type=MESH,
        )

    def obs3(d):
        peer = (za + d) % NZA
        return pltpu.make_async_remote_copy(
            oe.at[peer], og.at[za], os3.at[d - 1], or3.at[d - 1],
            device_id=dev(x=ya * NZA + peer), device_id_type=MESH,
        )

    for d in range(1, NTY):
        obs1(d).start()

    def halo(f, side):
        source, target, x = (1, NXC + 1, tx - 1) if side == 0 else (NXC, 0, tx + 1)
        return pltpu.make_async_remote_copy(
            ms.at[f, source], ms.at[f, target], hs_sem.at[side, f], hr_sem.at[side, f],
            device_id=dev(x=x), device_id_type=MESH,
        )

    def plane(f, x):
        for b in range(NB):
            r = x * NB + b
            ms[f, x + 1, b, 0:NL] = raw[f, pl.ds(r, NL, stride=STEP), :] * mask[r].astype(F32)

    def edges(f, carry):
        fetch(f).wait()
        plane(f, 0)
        plane(f, NXC - 1)

        @pl.when(has_left)
        def _():
            halo(f, 0).start()

        @pl.when(has_right)
        def _():
            halo(f, 1).start()

        return carry

    lax.fori_loop(0, NF, edges, 0)

    def planes(f, carry):
        first, last = carry
        for x in range(1, NXC - 1):
            plane(f, x)
        for x in range(NXC):
            here = lane == f * NXC + x
            first = jnp.where(here, ms[f, x + 1, 0, 0:NL, 0:1], first)
            last = jnp.where(here, ms[f, x + 1, NB - 1, 0:NL, 127:128], last)
        return first, last

    zero = jnp.zeros((NL, 128), F32)
    first, last = lax.fori_loop(0, NF, planes, (zero, zero))
    ycols[0, 0:NL] = first
    ycols[1, 0:NL] = last

    def yedge(side):
        return pltpu.make_async_remote_copy(
            ycols.at[side], yhalo.at[1 - side], ys_sem.at[side], yr_sem.at[side],
            device_id=dev(y=ty - 1 if side == 0 else ty + 1), device_id_type=MESH,
        )

    @pl.when(has_down)
    def _():
        yedge(0).start()

    @pl.when(has_up)
    def _():
        yedge(1).start()

    for d in range(1, NTY):
        obs1(d).wait_recv()
    ob[ty] = oa[pl.ds(pl.multiple_of(ty * NTX, NTX), NTX), :]
    for s in range(NTY):
        oc[:, s * SLOTS:(s + 1) * SLOTS] = ob[s, :, 0:SLOTS]
    for d in range(1, NYA):
        obs2(d).start()

    @pl.when(has_down)
    def _():
        yedge(1).wait_recv()

    @pl.when(has_up)
    def _():
        yedge(0).wait_recv()

    def feedback(f):
        return pltpu.make_async_remote_copy(
            pay.at[f], got.at[f], gs_sem.at[f], gr_sem.at[f],
            device_id=dev(g=1 - grp), device_id_type=MESH,
        )

    def keep(ref, i, value):
        high, low = split(value)
        ref[i * 64:i * 64 + NL] = high
        ref[256 + i * 64:256 + i * 64 + NL] = low

    def both(result, i):
        return result[i * 64:i * 64 + NL] + result[256 + i * 64:256 + i * 64 + NL]

    def advance(f, carry):
        @pl.when(has_left)
        def _():
            halo(f, 1).wait_recv()

        @pl.when(has_right)
        def _():
            halo(f, 0).wait_recv()

        turn = lax.rem(128 - f * NXC, 128)
        below = pltpu.roll(yhalo[0, 0:LP], turn, axis=1)
        above = pltpu.roll(yhalo[1, 0:LP], turn, axis=1)
        lanes = lax.broadcasted_iota(jnp.int32, (LP, 128), 1)
        for pair in range(NXC // 2):
            for half in range(2):
                x = 2 * pair + half
                cells = [ms[f, x + 1, b] for b in range(NB)]
                up = [pltpu.roll(c, 1, axis=1) for c in cells]
                down = [pltpu.roll(c, 127, axis=1) for c in cells]
                edge_low = below if x == 0 else pltpu.roll(below, 128 - x, axis=1)
                edge_high = pltpu.roll(above, 127 - x, axis=1)
                for b in range(NB):
                    prev = jnp.where(lanes == 0, up[b - 1] if b else edge_low, up[b])
                    after = jnp.where(lanes == 127, down[b + 1] if b < NB - 1 else edge_high, down[b])
                    beside = ms[f, x, b] + ms[f, x + 2, b] + prev + after
                    spread = cells[b] + kappa[x * NB + b] * (beside - 4.0 * cells[b])
                    high, low = split(spread[0:NL])
                    col = half * NYC + b * 128
                    xs[pair, 0:NL, col:col + 128] = high
                    xs[pair, 64:64 + NL, col:col + 128] = low
                    xs[pair, 128:128 + NL, col:col + 128] = high
            mixed = jnp.dot(mc[f], xs[pair], preferred_element_type=F32)
            mx[f, 2 * pair] = mixed[0:LP, 0:NYC]
            mx[f, 2 * pair + 1] = mixed[0:LP, NYC:]

        @pl.when(child)
        def _():
            for i in range(4):
                total = mx[f, 3 * i, 0:NL] * nudge[3 * i:3 * i + 1, :]
                for a in range(1, 3):
                    total = total + mx[f, 3 * i + a, 0:NL] * nudge[3 * i + a:3 * i + a + 1, :]
                keep(lhs, i, total)

        @pl.when(parent)
        def _():
            for i in range(4):
                keep(lhs, i, mx[f, nest_x[0] + i, 0:NL])

        picked = jnp.dot(lhs[...], wsel[...], preferred_element_type=F32)
        for i in range(4):
            pay[f, i, 0:NL] = both(picked, i)
        feedback(f).start()

        @pl.when(f == 1)
        def _():
            for d in range(1, NYA):
                obs2(d).wait_recv()
            own = pl.ds(pl.multiple_of(ya * NZA, NZA), NZA)
            od[own, :] = oc[own, :]
            for z in range(NZA):
                oe[z, 0:NYA] = od[pl.ds(z, NYA, stride=NZA), :]
            for d in range(1, NZA):
                obs3(d).start()

        return carry

    lax.fori_loop(0, NF, advance, 0)

    take = jnp.where(child, 1.0 / 9.0, 1.0)
    give = jnp.where(child, 0.0, 1.0)

    def finish(f, carry):
        feedback(f).wait_recv()
        for i in range(4):
            keep(dlt, i, got[f, i, 0:NL] * take - pay[f, i, 0:NL] * give)
        laid = jnp.dot(dlt[...], wback[...], preferred_element_type=F32)
        for i in range(4):
            cu[i, 0:NL] = both(laid, i)
        for x in range(NXC):
            p = x - nest_x[0]
            index = jnp.where(child, x // 3, jnp.where((p >= 0) & (p < 4), p, 4))
            done = mx[f, x, 0:NL] + cu[index, 0:NL]
            for b in range(NB):
                out[f, pl.ds(x * NB + b, NL, stride=STEP), :] = done[:, b * 128:(b + 1) * 128]
        return carry

    lax.fori_loop(0, NF, finish, 0)

    for d in range(1, NZA):
        obs3(d).wait_recv()
    og[za] = oe[za]
    for z in range(NZA):
        obs_out[z * 8:(z + 1) * 8, :] = og[z]

    for d in range(1, NTY):
        obs1(d).wait_send()
    for d in range(1, NYA):
        obs2(d).wait_send()
    for d in range(1, NZA):
        obs3(d).wait_send()

    @pl.when(has_left)
    def _():
        for f in range(NF):
            halo(f, 0).wait_send()

    @pl.when(has_right)
    def _():
        for f in range(NF):
            halo(f, 1).wait_send()

    @pl.when(has_down)
    def _():
        yedge(0).wait_send()

    @pl.when(has_up)
    def _():
        yedge(1).wait_send()

    for f in range(NF):
        feedback(f).wait_send()


def scatter_kernel(vals, cells, counts, start, mask, out, base, add0, add1, wide, in_sem, out_sem):
    incoming = pltpu.make_async_copy(start, base, in_sem)
    incoming.start()
    add0[...] = jnp.zeros_like(add0)
    add1[...] = jnp.zeros_like(add1)
    for r in range(2 * STEP):
        wide[r:r + 1, :] = mask[r % STEP].astype(F32)
    lane = lax.broadcasted_iota(jnp.int32, (1, 128), 1)

    def source(i, carry):
        z, y = i // NYA, i % NYA
        for t in range(NTY):
            s = t * NTX + y * NZA + z
            count = counts[0, s]
            for k in range(SLOTS):
                cell = cells[k, s]
                value = jnp.where(k < count, vals[z * 8 + y, t * SLOTS + k], 0.0)
                row = pl.ds(lax.shift_right_logical(cell, 7), 1)
                term = jnp.where(lane == (cell & 127), value, 0.0)
                ref = add1 if k % 2 else add0
                ref[row, :] = ref[row, :] + term
        return carry

    lax.fori_loop(0, NYA * NZA, source, 0)
    incoming.wait()

    def leave(f):
        rows = pl.ds(f * ROWS, ROWS)
        return pltpu.make_async_copy(base.at[rows], out.at[rows], out_sem.at[f])

    for f in range(NF):
        def masked(i, carry):
            rows = pl.ds(pl.multiple_of(f * ROWS + i * 2 * STEP, 8), 2 * STEP)
            base[rows, :] = wide[...] * (base[rows, :] + add0[rows, :] + add1[rows, :])
            return carry

        lax.fori_loop(0, ROWS // (2 * STEP), masked, 0)
        leave(f).start()
    for f in range(NF):
        leave(f).wait()


VM = pl.BlockSpec(memory_space=pltpu.VMEM)
SM = pl.BlockSpec(memory_space=pltpu.SMEM)
ANY = pl.BlockSpec(memory_space=pl.ANY)
DMA = pltpu.SemaphoreType.DMA


def local(
    adjoint_state, land_mask, diffusivity, mixing, nudging, nest_x, nest_y, obs_forcing, obs_cell, obs_count
):
    state = adjoint_state.reshape(NF, ROWS, 128)
    mask = land_mask.reshape(STEP, 1, 128)
    kappa = diffusivity.reshape(STEP, 1, 128)
    cells = jnp.transpose(obs_cell[0, :, :, 0])
    counts = obs_count[0, :, 0].reshape(1, -1)
    scratch = [
        pltpu.VMEM((NF, ROWS, 128), F32),
        pltpu.VMEM((NF, NXC + 2, NB, LP, 128), F32),
        pltpu.VMEM((NXC // 2, 192, 2 * NYC), BF16),
        pltpu.VMEM((NF, 64, 192), BF16),
        pltpu.VMEM((NF, NXC, LP, NYC), F32),
        pltpu.VMEM((NYC, 128), BF16),
        pltpu.VMEM((128, NYC), BF16),
        pltpu.VMEM((512, NYC), BF16),
        pltpu.VMEM((NF, 4, LP, 128), F32),
        pltpu.VMEM((NF, 4, LP, 128), F32),
        pltpu.VMEM((512, 128), BF16),
        pltpu.VMEM((5, LP, NYC), F32),
        pltpu.VMEM((2, LP, 128), F32),
        pltpu.VMEM((2, LP, 128), F32),
        pltpu.VMEM((128, 128), F32),
        pltpu.VMEM((NTY, NTX, 128), F32),
        pltpu.VMEM((NTX, 128), F32),
        pltpu.VMEM((NTX, 128), F32),
        pltpu.VMEM((NZA, 8, 128), F32),
        pltpu.VMEM((NZA, 8, 128), F32),
        DMA((NF,)), DMA((2, NF)), DMA((2, NF)), DMA((2,)), DMA((2,)), DMA((NF,)), DMA((NF,)),
        DMA((NTY - 1,)), DMA((NTY - 1,)), DMA((NYA - 1,)), DMA((NYA - 1,)), DMA((NZA - 1,)), DMA((NZA - 1,)),
    ]
    partial, arrived = pl.pallas_call(
        exchange_kernel,
        out_shape=(
            jax.ShapeDtypeStruct((NF, ROWS, 128), F32),
            jax.ShapeDtypeStruct((NZA * 8, 128), F32),
        ),
        in_specs=[SM, SM, ANY, VM, VM, VM, VM, VM],
        out_specs=(VM, VM),
        scratch_shapes=scratch,
        compiler_params=pltpu.CompilerParams(
            collective_id=0, has_side_effects=True, vmem_limit_bytes=44 * 2**20
        ),
        name="exchange",
    )(nest_x, nest_y, state, mask, kappa, nudging, mixing[0], obs_forcing[0, 0])
    total = NF * ROWS
    result = pl.pallas_call(
        scatter_kernel,
        out_shape=jax.ShapeDtypeStruct((total, 128), F32),
        in_specs=[SM, SM, SM, ANY, VM],
        out_specs=ANY,
        scratch_shapes=[
            pltpu.VMEM((total, 128), F32), pltpu.VMEM((total, 128), F32), pltpu.VMEM((total, 128), F32),
            pltpu.VMEM((2 * STEP, 128), F32), DMA, DMA((NF,)),
        ],
        compiler_params=pltpu.CompilerParams(vmem_limit_bytes=24 * 2**20),
        name="scatter",
    )(arrived, cells, counts, partial.reshape(total, 128), mask)
    return result.reshape(1, NF, NL, NXC, NYC)


def solution(mesh):
    in_specs = (
        P("grp", None, None, "tx", "ty"),
        P("grp", "tx", "ty"),
        P("grp", "tx", "ty"),
        P("grp", None, None, None),
        P("tx", "ty"),
        P(("ty", "tx")),
        P(("ty", "tx")),
        P("grp", ("ty", "tx"), None, None),
        P("grp", None, None, ("ty", "tx")),
        P("grp", None, ("ty", "tx")),
    )
    out_specs = P("grp", None, None, "tx", "ty")
    return jax.shard_map(local, mesh=mesh, in_specs=in_specs, out_specs=out_specs, check_vma=False)
```

time: 193 us -> 53.6 us (0.28)
  the two profiles are of different devices: /device:TPU:25 before, /device:TPU:1 now
where the time goes in v1:
time: 53.6 us; the launch traced here: 53.2 us
  Pallas kernels  45.8 us (85%)
  local copies, waits for them, and re-layouts  6.1 us (11%)
  between operations  1.37 us (3%)
    pallas_call x1, Pallas kernels, local(): pl.pallas_call(exchange_kernel, out_shape=(jax.ShapeDtypeStruct((NF, ROWS...  35.1 us
    pallas_call x1, Pallas kernels, local(): pl.pallas_call(scatter_kernel, out_shape=jax.ShapeDtypeStruct((total, 128...  10.7 us
    unnamed x15, local copies, waits for them, and re-layouts  6.1 us

profile of v1, /device:TPU:1, one launch (start us, length us, event | category | flops | bytes accessed | tf_op | source)
XLA Modules:
  0.0 53.2 jit_solution(2140871397402575170)
XLA Ops:
  0.0 0.0 copy-start.6
  0.0 0.0 copy-start.5
  1.3 0.9 %copy.15 = f32[1,5,50,50]{3,2,0,1:T(8,128)S(1)} copy(f32[1,5,50,50]{3,0,2,1:T(1,128)} %param.13) | data formatting | bytes 100000
  2.2 0.0 copy-start
  2.3 2.3 %copy-done = f32[1,5,50,12,384]{4,0,3,2,1:T(1,128)S(1)} copy-done((f32[1,5,50,12,384]{4,0,3,2,1:T(1,128)S(1)}, f32[1,5,50,12,384]{4,0,3,2,1:T(1,128)}, u32[]{:S(2)}) %copy-start) | copy-done | bytes 4608024
  4.6 0.0 copy-start.1
  4.6 0.7 %copy-done.1 = s32[1,12,384]{2,0,1:T(1,128)S(1)} copy-done((s32[1,12,384]{2,0,1:T(1,128)S(1)}, s32[1,12,384]{2,0,1:T(1,128)}, u32[]{:S(2)}) %copy-start.1) | copy-done | bytes 18456
  5.3 0.0 copy-start.2
  5.3 0.7 %copy-done.2 = f32[12,384]{1,0:T(8,128)S(1)} copy-done((f32[12,384]{1,0:T(8,128)S(1)}, f32[12,384]{1,0:T(8,128)}, u32[]{:S(2)}) %copy-start.2) | copy-done | bytes 18456
  6.0 0.0 copy-start.3
  6.0 0.7 %copy-done.3 = f32[1,12,384]{2,0,1:T(1,128)S(1)} copy-done((f32[1,12,384]{2,0,1:T(1,128)S(1)}, f32[1,12,384]{2,0,1:T(1,128)}, u32[]{:S(2)}) %copy-start.3) | copy-done | bytes 18456
  6.7 0.0 copy-start.4
  6.7 0.7 %copy-done.4 = f32[1,1,16,128]{3,2,1,0:T(8,128)S(1)} copy-done((f32[1,1,16,128]{3,2,1,0:T(8,128)S(1)}, f32[1,1,16,128]{3,2,1,0:T(8,128)}, u32[]{:S(2)}) %copy-start.4) | copy-done | bytes 8216
  7.4 35.1 %exchange.1 = (f32[5,1800,128]{2,1,0:T(8,128)S(1)}, f32[64,128]{1,0:T(8,128)S(1)}) custom-call(s32[1]{0:T(128)S(6)} %copy.16.nest_x, s32[1]{0:T(128)S(6)} %copy.17.nest_y, f32[5,1800,128]{2,1,0:T(8,128)S(1)} %bitcast.13, s32[36,1,128]{2,1,0:T(1,128)S(1)} %bitcast.16, f32[36,1,128]{2,1,0:T(1,128)S(1)} %bitcast.18, f32[12,384]{1,0:T(8,128)S(1)} %copy-done.2, ...), custom_call_target="tpu_custom_call" | custom-call | tf_op jit(solution)/shard_map/exchange/pallas_call | solution.py:436
  42.5 0.0 copy-done.6
  42.5 0.0 copy-done.5
  42.5 10.7 %scatter.1 = f32[9000,128]{1,0:T(8,128)} custom-call(f32[64,128]{1,0:T(8,128)S(1)} %get-tuple-element.7.vals, s32[16,128]{1,0:T(8,128)S(1)} %bitcast.20, s32[1,128]{1,0:T(1,128)S(1)} %bitcast.21, f32[9000,128]{1,0:T(8,128)S(1)} %bitcast.14, s32[36,1,128]{2,1,0:T(1,128)S(1)} %bitcast.17), custom_call_target="tpu_custom_call" | custom-call | tf_op jit(solution)/shard_map/scatter/pallas_call | solution.py:451
Async XLA Ops:
  0.0 42.5 %copy-start.6 = (s32[1,128,1]{1,2,0:T(1,128)S(1)}, s32[1,128,1]{1,2,0:T(1,128)}, u32[]{:S(2)}) copy-start(s32[1,128,1]{1,2,0:T(1,128)} %param.19) | copy-start | bytes 1540
  0.0 42.5 %copy-start.5 = (s32[1,128,16,1]{1,3,2,0:T(1,128)S(1)}, s32[1,128,16,1]{1,3,2,0:T(1,128)}, u32[]{:S(2)}) copy-start(s32[1,128,16,1]{1,3,2,0:T(1,128)} %param.18) | copy-start | bytes 24580
  2.2 2.3 %copy-start = (f32[1,5,50,12,384]{4,0,3,2,1:T(1,128)S(1)}, f32[1,5,50,12,384]{4,0,3,2,1:T(1,128)}, u32[]{:S(2)}) copy-start(f32[1,5,50,12,384]{4,0,3,2,1:T(1,128)} %param.10) | copy-start | bytes 13824004
  4.6 0.7 %copy-start.1 = (s32[1,12,384]{2,0,1:T(1,128)S(1)}, s32[1,12,384]{2,0,1:T(1,128)}, u32[]{:S(2)}) copy-start(s32[1,12,384]{2,0,1:T(1,128)} %param.11) | copy-start | bytes 55300
  5.3 0.7 %copy-start.2 = (f32[12,384]{1,0:T(8,128)S(1)}, f32[12,384]{1,0:T(8,128)}, u32[]{:S(2)}) copy-start(f32[12,384]{1,0:T(8,128)} %nudge.1) | copy-start | bytes 55300
  6.0 0.7 %copy-start.3 = (f32[1,12,384]{2,0,1:T(1,128)S(1)}, f32[1,12,384]{2,0,1:T(1,128)}, u32[]{:S(2)}) copy-start(f32[1,12,384]{2,0,1:T(1,128)} %param.12) | copy-start | bytes 55300
  6.7 0.7 %copy-start.4 = (f32[1,1,16,128]{3,2,1,0:T(8,128)S(1)}, f32[1,1,16,128]{3,2,1,0:T(8,128)}, u32[]{:S(2)}) copy-start(f32[1,1,16,128]{3,2,1,0:T(8,128)} %param.17) | copy-start | bytes 24580

commit v2 on v1

--- a/solution.py
+++ b/solution.py
@@ -17,6 +17,8 @@
 STEP = NXC * NB
 NTY, NTX, NYA, NZA = 4, 32, 4, 8
 SLOTS = 16
+AHEAD = 2
+VMEM_BYTES = 63 * 2**20
 
 
 def split(value):
@@ -26,12 +28,13 @@
 
 
 def exchange_kernel(
-    nest_x, nest_y, state, mask, kappa, nudge, mix, obs,
+    nest_x_in, nest_y_in, state, mask_in, kappa_in, nudge_in, mix_in, obs_in,
     out, obs_out,
+    nest_x, nest_y, mask, kappa, nudge, mix, obs, packed,
     raw, ms, xs, mc, mx, wsel, wback, lhs, pay, got, dlt, cu,
     ycols, yhalo, oa, ob, oc, od, oe, og,
     in_sem, hs_sem, hr_sem, ys_sem, yr_sem, gs_sem, gr_sem,
-    os1, or1, os2, or2, os3, or3,
+    os1, or1, os2, or2, os3, or3, small_sem, far_sem, out_sem,
 ):
     grp = lax.axis_index("grp")
     ty = lax.axis_index("ty")
@@ -46,8 +49,19 @@
     def fetch(f):
         return pltpu.make_async_copy(state.at[f], raw.at[f], in_sem.at[f])
 
+    smalls = [
+        pltpu.make_async_copy(source, target, small_sem.at[i])
+        for i, (source, target) in enumerate(
+            [(obs_in, obs), (mask_in, mask), (mix_in, mix), (nest_x_in, nest_x), (nest_y_in, nest_y),
+             (kappa_in, kappa), (nudge_in, nudge)]
+        )
+    ]
+    smalls[0].start()
+    smalls[1].start()
     for f in range(NF):
         fetch(f).start()
+    for copy in smalls[2:]:
+        copy.start()
 
     barrier = pltpu.get_barrier_semaphore()
 
@@ -56,22 +70,37 @@
 
     has_left, has_right = tx > 0, tx < NTX - 1
     has_down, has_up = ty > 0, ty < NTY - 1
+    ring = (
+        dev(y=(ty + 1) % NTY), dev(y=(ty + 3) % NTY),
+        dev(x=((ya + 1) % NYA) * NZA + za), dev(x=((ya + 3) % NYA) * NZA + za),
+        dev(x=ya * NZA + (za + 1) % NZA), dev(x=ya * NZA + (za + 7) % NZA),
+    )
     greet(dev(g=1 - grp))
-    for d in range(1, NTY):
-        greet(dev(y=(ty + d) % NTY))
-    for d in range(1, NYA):
-        greet(dev(x=((ya + d) % NYA) * NZA + za))
-    for d in range(1, NZA):
-        greet(dev(x=ya * NZA + (za + d) % NZA))
-
-    @pl.when(has_left)
+    for device in ring:
+        greet(device)
+    wrap_left = (za == 0) & has_left
+    wrap_right = (za == NZA - 1) & has_right
+
+    @pl.when(wrap_left)
     def _():
         greet(dev(x=tx - 1))
 
-    @pl.when(has_right)
+    @pl.when(wrap_right)
     def _():
         greet(dev(x=tx + 1))
 
+    def vouch(stage, sides):
+        for side in sides:
+            pl.semaphore_signal(
+                far_sem.at[stage, side], inc=1, device_id=ring[side], device_id_type=MESH
+            )
+
+    def vouched(stage, sides):
+        for side in sides:
+            pl.semaphore_wait(far_sem.at[stage, side], 1)
+
+    for copy in smalls:
+        copy.wait()
     oa[:, 0:SLOTS] = obs[...].T
     lane = lax.broadcasted_iota(jnp.int32, (NL, 128), 1)
     scale = jnp.where(child, 3, 1)
@@ -87,7 +116,7 @@
     mc[...] = jnp.zeros_like(mc)
     xs[...] = jnp.zeros_like(xs)
     for f in range(NF):
-        high, low = split(mix[f])
+        high, low = split(mix[f, :, 0, :])
         mc[f, 0:NL, 0:NL] = high
         mc[f, 0:NL, 64:64 + NL] = high
         mc[f, 0:NL, 128:128 + NL] = low
@@ -112,10 +141,8 @@
     def _():
         yhalo[1] = jnp.zeros(yhalo.shape[1:], F32)
 
-    pl.semaphore_wait(
-        barrier,
-        1 + (NTY - 1) + (NYA - 1) + (NZA - 1) + jnp.where(has_left, 1, 0) + jnp.where(has_right, 1, 0),
-    )
+    pl.semaphore_wait(barrier, 1 + len(ring) + jnp.where(wrap_left | wrap_right, 1, 0))
+    vouch(0, range(6))
 
     def obs1(d):
         peer = (ty + d) % NTY
@@ -139,15 +166,21 @@
             device_id=dev(x=ya * NZA + peer), device_id_type=MESH,
         )
 
-    for d in range(1, NTY):
-        obs1(d).start()
-
     def halo(f, side):
         source, target, x = (1, NXC + 1, tx - 1) if side == 0 else (NXC, 0, tx + 1)
         return pltpu.make_async_remote_copy(
-            ms.at[f, source], ms.at[f, target], hs_sem.at[side, f], hr_sem.at[side, f],
+            ms.at[f, source, :, pl.ds(0, NL)], ms.at[f, target, :, pl.ds(0, NL)], hs_sem.at[side, f], hr_sem.at[side, f],
             device_id=dev(x=x), device_id_type=MESH,
         )
+
+    def send_halo(f):
+        @pl.when(has_left)
+        def _():
+            halo(f, 0).start()
+
+        @pl.when(has_right)
+        def _():
+            halo(f, 1).start()
 
     def plane(f, x):
         for b in range(NB):
@@ -159,13 +192,9 @@
         plane(f, 0)
         plane(f, NXC - 1)
 
-        @pl.when(has_left)
-        def _():
-            halo(f, 0).start()
-
-        @pl.when(has_right)
-        def _():
-            halo(f, 1).start()
+        @pl.when(f < AHEAD)
+        def _():
+            send_halo(f)
 
         return carry
 
@@ -188,7 +217,7 @@
 
     def yedge(side):
         return pltpu.make_async_remote_copy(
-            ycols.at[side], yhalo.at[1 - side], ys_sem.at[side], yr_sem.at[side],
+            ycols.at[side, pl.ds(0, NL)], yhalo.at[1 - side, pl.ds(0, NL)], ys_sem.at[side], yr_sem.at[side],
             device_id=dev(y=ty - 1 if side == 0 else ty + 1), device_id_type=MESH,
         )
 
@@ -200,13 +229,10 @@
     def _():
         yedge(1).start()
 
+    vouched(0, range(6))
+    vouch(1, (4, 5))
     for d in range(1, NTY):
-        obs1(d).wait_recv()
-    ob[ty] = oa[pl.ds(pl.multiple_of(ty * NTX, NTX), NTX), :]
-    for s in range(NTY):
-        oc[:, s * SLOTS:(s + 1) * SLOTS] = ob[s, :, 0:SLOTS]
-    for d in range(1, NYA):
-        obs2(d).start()
+        obs1(d).start()
 
     @pl.when(has_down)
     def _():
@@ -218,7 +244,7 @@
 
     def feedback(f):
         return pltpu.make_async_remote_copy(
-            pay.at[f], got.at[f], gs_sem.at[f], gr_sem.at[f],
+            pay.at[f, :, pl.ds(0, NL)], got.at[f, :, pl.ds(0, NL)], gs_sem.at[f], gr_sem.at[f],
             device_id=dev(g=1 - grp), device_id_type=MESH,
         )
 
@@ -231,6 +257,10 @@
         return result[i * 64:i * 64 + NL] + result[256 + i * 64:256 + i * 64 + NL]
 
     def advance(f, carry):
+        @pl.when(f + AHEAD < NF)
+        def _():
+            send_halo(f + AHEAD)
+
         @pl.when(has_left)
         def _():
             halo(f, 1).wait_recv()
@@ -283,8 +313,21 @@
             pay[f, i, 0:NL] = both(picked, i)
         feedback(f).start()
 
-        @pl.when(f == 1)
-        def _():
+        @pl.when(f == 0)
+        def _():
+            vouched(1, (4, 5))
+            vouch(2, (4, 5))
+            for d in range(1, NTY):
+                obs1(d).wait_recv()
+            ob[ty] = oa[pl.ds(pl.multiple_of(ty * NTX, NTX), NTX), :]
+            for s in range(NTY):
+                oc[:, s * SLOTS:(s + 1) * SLOTS] = ob[s, :, 0:SLOTS]
+            for d in range(1, NYA):
+                obs2(d).start()
+
+        @pl.when(f == 2)
+        def _():
+            vouched(2, (4, 5))
             for d in range(1, NYA):
                 obs2(d).wait_recv()
             own = pl.ds(pl.multiple_of(ya * NZA, NZA), NZA)
@@ -313,8 +356,12 @@
             index = jnp.where(child, x // 3, jnp.where((p >= 0) & (p < 4), p, 4))
             done = mx[f, x, 0:NL] + cu[index, 0:NL]
             for b in range(NB):
-                out[f, pl.ds(x * NB + b, NL, stride=STEP), :] = done[:, b * 128:(b + 1) * 128]
+                raw[f, pl.ds(x * NB + b, NL, stride=STEP), :] = done[:, b * 128:(b + 1) * 128]
+        leave(f).start()
         return carry
+
+    def leave(f):
+        return pltpu.make_async_copy(raw.at[f], out.at[f], out_sem.at[f])
 
     lax.fori_loop(0, NF, finish, 0)
 
@@ -322,7 +369,9 @@
         obs3(d).wait_recv()
     og[za] = oe[za]
     for z in range(NZA):
-        obs_out[z * 8:(z + 1) * 8, :] = og[z]
+        packed[z * 8:(z + 1) * 8, :] = og[z]
+    leave_obs = pltpu.make_async_copy(packed, obs_out, out_sem.at[NF])
+    leave_obs.start()
 
     for d in range(1, NTY):
         obs1(d).wait_send()
@@ -351,42 +400,57 @@
 
     for f in range(NF):
         feedback(f).wait_send()
-
-
-def scatter_kernel(vals, cells, counts, start, mask, out, base, add0, add1, wide, in_sem, out_sem):
-    incoming = pltpu.make_async_copy(start, base, in_sem)
-    incoming.start()
+        leave(f).wait()
+    leave_obs.wait()
+
+
+def scatter_kernel(
+    vals_in, cells_in, counts_in, start_in, mask_in,
+    out, vals, cells, counts, start, mask, terms, wide, index, add0, add1, in_sem, out_sem,
+):
+    fetches = [
+        pltpu.make_async_copy(source, target, in_sem.at[i])
+        for i, (source, target) in enumerate(
+            [(vals_in, vals), (cells_in, cells), (counts_in, counts), (mask_in, mask), (cells_in, index), (start_in, start)]
+        )
+    ]
+    for fetch in fetches:
+        fetch.start()
     add0[...] = jnp.zeros_like(add0)
     add1[...] = jnp.zeros_like(add1)
+    for fetch in fetches[:5]:
+        fetch.wait()
     for r in range(2 * STEP):
         wide[r:r + 1, :] = mask[r % STEP].astype(F32)
-    lane = lax.broadcasted_iota(jnp.int32, (1, 128), 1)
+    slot = lax.broadcasted_iota(jnp.int32, (SLOTS, 128), 0)
+    lane = lax.broadcasted_iota(jnp.int32, (SLOTS, 128), 1)
+    lanes = jnp.where(slot < counts[...], cells[...] & 127, -1)
+    turned = vals[...].T
+    for s in range(NTY * NTX):
+        t, y, z = s // NTX, s % NTX // NZA, s % NZA
+        value = turned[t * SLOTS:(t + 1) * SLOTS, z * 8 + y:z * 8 + y + 1]
+        terms[s * SLOTS:(s + 1) * SLOTS, :] = jnp.where(lane == lanes[:, s:s + 1], value, 0.0)
 
     def source(i, carry):
-        z, y = i // NYA, i % NYA
-        for t in range(NTY):
-            s = t * NTX + y * NZA + z
-            count = counts[0, s]
+        for u in range(4):
+            s = i * 4 + u
             for k in range(SLOTS):
-                cell = cells[k, s]
-                value = jnp.where(k < count, vals[z * 8 + y, t * SLOTS + k], 0.0)
-                row = pl.ds(lax.shift_right_logical(cell, 7), 1)
-                term = jnp.where(lane == (cell & 127), value, 0.0)
+                row = pl.ds(lax.shift_right_logical(index[k, s], 7), 1)
                 ref = add1 if k % 2 else add0
-                ref[row, :] = ref[row, :] + term
+                ref[row, :] = ref[row, :] + terms[pl.ds(s * SLOTS + k, 1), :]
         return carry
 
-    lax.fori_loop(0, NYA * NZA, source, 0)
-    incoming.wait()
+    lax.fori_loop(0, NTY * NTX // 4, source, 0)
+    fetches[5].wait()
 
     def leave(f):
         rows = pl.ds(f * ROWS, ROWS)
-        return pltpu.make_async_copy(base.at[rows], out.at[rows], out_sem.at[f])
+        return pltpu.make_async_copy(add0.at[rows], out.at[rows], out_sem.at[f])
 
     for f in range(NF):
         def masked(i, carry):
             rows = pl.ds(pl.multiple_of(f * ROWS + i * 2 * STEP, 8), 2 * STEP)
-            base[rows, :] = wide[...] * (base[rows, :] + add0[rows, :] + add1[rows, :])
+            add0[rows, :] = wide[...] * (start[rows, :] + add0[rows, :] + add1[rows, :])
             return carry
 
         lax.fori_loop(0, ROWS // (2 * STEP), masked, 0)
@@ -395,9 +459,7 @@
         leave(f).wait()
 
 
-VM = pl.BlockSpec(memory_space=pltpu.VMEM)
-SM = pl.BlockSpec(memory_space=pltpu.SMEM)
-ANY = pl.BlockSpec(memory_space=pl.ANY)
+HBM = pl.BlockSpec(memory_space=pltpu.HBM)
 DMA = pltpu.SemaphoreType.DMA
 
 
@@ -410,6 +472,14 @@
     cells = jnp.transpose(obs_cell[0, :, :, 0])
     counts = obs_count[0, :, 0].reshape(1, -1)
     scratch = [
+        pltpu.SMEM((1,), jnp.int32),
+        pltpu.SMEM((1,), jnp.int32),
+        pltpu.VMEM((STEP, 1, 128), jnp.int32),
+        pltpu.VMEM((STEP, 1, 128), F32),
+        pltpu.VMEM((NXC, NYC), F32),
+        pltpu.VMEM((NF, NL, 1, NL), F32),
+        pltpu.VMEM((SLOTS, 128), F32),
+        pltpu.VMEM((NZA * 8, 128), F32),
         pltpu.VMEM((NF, ROWS, 128), F32),
         pltpu.VMEM((NF, NXC + 2, NB, LP, 128), F32),
         pltpu.VMEM((NXC // 2, 192, 2 * NYC), BF16),
@@ -432,6 +502,7 @@
         pltpu.VMEM((NZA, 8, 128), F32),
         DMA((NF,)), DMA((2, NF)), DMA((2, NF)), DMA((2,)), DMA((2,)), DMA((NF,)), DMA((NF,)),
         DMA((NTY - 1,)), DMA((NTY - 1,)), DMA((NYA - 1,)), DMA((NYA - 1,)), DMA((NZA - 1,)), DMA((NZA - 1,)),
+        DMA((7,)), pltpu.SemaphoreType.REGULAR((3, 6)), DMA((NF + 1,)),
     ]
     partial, arrived = pl.pallas_call(
         exchange_kernel,
@@ -439,25 +510,28 @@
             jax.ShapeDtypeStruct((NF, ROWS, 128), F32),
             jax.ShapeDtypeStruct((NZA * 8, 128), F32),
         ),
-        in_specs=[SM, SM, ANY, VM, VM, VM, VM, VM],
-        out_specs=(VM, VM),
+        in_specs=[HBM] * 8,
+        out_specs=(HBM, HBM),
         scratch_shapes=scratch,
         compiler_params=pltpu.CompilerParams(
-            collective_id=0, has_side_effects=True, vmem_limit_bytes=44 * 2**20
+            collective_id=0, has_side_effects=True, vmem_limit_bytes=VMEM_BYTES
         ),
         name="exchange",
-    )(nest_x, nest_y, state, mask, kappa, nudging, mixing[0], obs_forcing[0, 0])
+    )(nest_x, nest_y, state, mask, kappa, nudging, mixing.reshape(NF, NL, 1, NL), obs_forcing[0, 0])
     total = NF * ROWS
     result = pl.pallas_call(
         scatter_kernel,
         out_shape=jax.ShapeDtypeStruct((total, 128), F32),
-        in_specs=[SM, SM, SM, ANY, VM],
-        out_specs=ANY,
+        in_specs=[HBM] * 5,
+        out_specs=HBM,
         scratch_shapes=[
-            pltpu.VMEM((total, 128), F32), pltpu.VMEM((total, 128), F32), pltpu.VMEM((total, 128), F32),
-            pltpu.VMEM((2 * STEP, 128), F32), DMA, DMA((NF,)),
+            pltpu.VMEM((NZA * 8, 128), F32), pltpu.VMEM((SLOTS, NTY * NTX), jnp.int32),
+            pltpu.VMEM((1, NTY * NTX), jnp.int32), pltpu.VMEM((total, 128), F32), pltpu.VMEM((STEP, 1, 128), jnp.int32),
+            pltpu.VMEM((NTY * NTX * SLOTS, 128), F32), pltpu.VMEM((2 * STEP, 128), F32),
+            pltpu.SMEM((SLOTS, NTY * NTX), jnp.int32),
+            pltpu.VMEM((total, 128), F32), pltpu.VMEM((total, 128), F32), DMA((6,)), DMA((NF,)),
         ],
-        compiler_params=pltpu.CompilerParams(vmem_limit_bytes=24 * 2**20),
+        compiler_params=pltpu.CompilerParams(vmem_limit_bytes=VMEM_BYTES),
         name="scatter",
     )(arrived, cells, counts, partial.reshape(total, 128), mask)
     return result.reshape(1, NF, NL, NXC, NYC)

time: 53.6 us -> 40 us (0.75)
  the two profiles are of different devices: /device:TPU:1 before, /device:TPU:25 now
where the time goes in v2:
time: 40 us; the launch traced here: 39.9 us
  Pallas kernels  38.6 us (96%)
  between operations  1.3 us (3%)
    pallas_call x1, Pallas kernels, local(): pl.pallas_call(exchange_kernel, out_shape=(jax.ShapeDtypeStruct((NF, ROWS...  29.3 us
    pallas_call x1, Pallas kernels, local(): pl.pallas_call(scatter_kernel, out_shape=jax.ShapeDtypeStruct((total, 128...  9.26 us

profile of v2, /device:TPU:25, one launch (start us, length us, event | category | flops | bytes accessed | tf_op | source)
XLA Modules:
  0.0 39.9 jit_solution(2166331919041219291)
XLA Ops:
  1.3 29.3 %exchange.1 = (f32[5,1800,128]{2,1,0:T(8,128)}, f32[64,128]{1,0:T(8,128)}) custom-call(s32[1]{0:T(128)S(6)} %copy.13.nest_x_in, s32[1]{0:T(128)S(6)} %copy.14.nest_y_in, f32[5,1800,128]{2,1,0:T(8,128)} %bitcast.11, s32[36,1,128]{2,1,0:T(1,128)} %bitcast.14, f32[36,1,128]{2,1,0:T(1,128)} %bitcast.16, f32[12,384]{1,0:T(8,128)} %nudge_in.1, ...), custom_call_target="tpu_custom_call" | custom-call | tf_op jit(solution)/shard_map/exchange/pallas_call | solution.py:507
  30.6 9.3 %scatter.1 = f32[9000,128]{1,0:T(8,128)} custom-call(f32[64,128]{1,0:T(8,128)} %get-tuple-element.7.vals_in, s32[16,128]{1,0:T(8,128)} %bitcast.18, s32[1,128]{1,0:T(1,128)} %bitcast.19, f32[9000,128]{1,0:T(8,128)} %bitcast.12, s32[36,1,128]{2,1,0:T(1,128)} %bitcast.15), custom_call_target="tpu_custom_call" | custom-call | tf_op jit(solution)/shard_map/scatter/pallas_call | solution.py:522

commit v3 on v2

--- a/solution.py
+++ b/solution.py
@@ -121,7 +121,6 @@
         mc[f, 0:NL, 64:64 + NL] = high
         mc[f, 0:NL, 128:128 + NL] = low
     cu[4] = jnp.zeros(cu.shape[1:], F32)
-    ycols[...] = jnp.zeros_like(ycols)
 
     @pl.when(tx == 0)
     def _():
@@ -135,14 +134,13 @@
 
     @pl.when(ty == 0)
     def _():
-        yhalo[0] = jnp.zeros(yhalo.shape[1:], F32)
+        for part in range(2):
+            yhalo[part, 0] = jnp.zeros(yhalo.shape[2:], F32)
 
     @pl.when(ty == NTY - 1)
     def _():
-        yhalo[1] = jnp.zeros(yhalo.shape[1:], F32)
-
-    pl.semaphore_wait(barrier, 1 + len(ring) + jnp.where(wrap_left | wrap_right, 1, 0))
-    vouch(0, range(6))
+        for part in range(2):
+            yhalo[part, 1] = jnp.zeros(yhalo.shape[2:], F32)
 
     def obs1(d):
         peer = (ty + d) % NTY
@@ -187,7 +185,53 @@
             r = x * NB + b
             ms[f, x + 1, b, 0:NL] = raw[f, pl.ds(r, NL, stride=STEP), :] * mask[r].astype(F32)
 
-    def edges(f, carry):
+    def columns(f, shift, first, last):
+        for x in range(NXC):
+            here = lane == shift + x
+            first = jnp.where(here, ms[f, x + 1, 0, 0:NL, 0:1], first)
+            last = jnp.where(here, ms[f, x + 1, NB - 1, 0:NL, 127:128], last)
+        return first, last
+
+    def yedge(part, side):
+        return pltpu.make_async_remote_copy(
+            ycols.at[part, side, pl.ds(0, NL)], yhalo.at[part, 1 - side, pl.ds(0, NL)],
+            ys_sem.at[part, side], yr_sem.at[part, side],
+            device_id=dev(y=ty - 1 if side == 0 else ty + 1), device_id_type=MESH,
+        )
+
+    def send_columns(part, first, last):
+        ycols[part, 0, 0:NL] = first
+        ycols[part, 1, 0:NL] = last
+
+        @pl.when(has_down)
+        def _():
+            yedge(part, 0).start()
+
+        @pl.when(has_up)
+        def _():
+            yedge(part, 1).start()
+
+    def await_columns(part):
+        @pl.when(has_down)
+        def _():
+            yedge(part, 1).wait_recv()
+
+        @pl.when(has_up)
+        def _():
+            yedge(part, 0).wait_recv()
+
+    zero = jnp.zeros((NL, 128), F32)
+    fetch(0).wait()
+    for x in (0, NXC - 1, *range(1, NXC - 1)):
+        plane(0, x)
+    first, last = columns(0, 0, zero, zero)
+    pl.semaphore_wait(barrier, 1 + len(ring) + jnp.where(wrap_left | wrap_right, 1, 0))
+    send_columns(0, first, last)
+    send_halo(0)
+    vouch(0, range(6))
+
+    def planes(f, carry):
+        first, last = carry
         fetch(f).wait()
         plane(f, 0)
         plane(f, NXC - 1)
@@ -196,122 +240,100 @@
         def _():
             send_halo(f)
 
-        return carry
-
-    lax.fori_loop(0, NF, edges, 0)
-
-    def planes(f, carry):
-        first, last = carry
         for x in range(1, NXC - 1):
             plane(f, x)
-        for x in range(NXC):
-            here = lane == f * NXC + x
-            first = jnp.where(here, ms[f, x + 1, 0, 0:NL, 0:1], first)
-            last = jnp.where(here, ms[f, x + 1, NB - 1, 0:NL, 127:128], last)
-        return first, last
-
-    zero = jnp.zeros((NL, 128), F32)
-    first, last = lax.fori_loop(0, NF, planes, (zero, zero))
-    ycols[0, 0:NL] = first
-    ycols[1, 0:NL] = last
-
-    def yedge(side):
-        return pltpu.make_async_remote_copy(
-            ycols.at[side, pl.ds(0, NL)], yhalo.at[1 - side, pl.ds(0, NL)], ys_sem.at[side], yr_sem.at[side],
-            device_id=dev(y=ty - 1 if side == 0 else ty + 1), device_id_type=MESH,
-        )
-
-    @pl.when(has_down)
-    def _():
-        yedge(0).start()
-
-    @pl.when(has_up)
-    def _():
-        yedge(1).start()
+        return columns(f, (f - 1) * NXC, first, last)
+
+    first, last = lax.fori_loop(1, NF, planes, (zero, zero))
+    send_columns(1, first, last)
 
     vouched(0, range(6))
     vouch(1, (4, 5))
     for d in range(1, NTY):
         obs1(d).start()
 
-    @pl.when(has_down)
-    def _():
-        yedge(1).wait_recv()
-
-    @pl.when(has_up)
-    def _():
-        yedge(0).wait_recv()
-
-    def feedback(f):
+    def feedback(f, part):
+        planes = pl.ds(2 * part, 2)
         return pltpu.make_async_remote_copy(
-            pay.at[f, :, pl.ds(0, NL)], got.at[f, :, pl.ds(0, NL)], gs_sem.at[f], gr_sem.at[f],
+            pay.at[f, planes, pl.ds(0, NL)], got.at[f, planes, pl.ds(0, NL)],
+            gs_sem.at[part, f], gr_sem.at[part, f],
             device_id=dev(g=1 - grp), device_id_type=MESH,
         )
 
-    def keep(ref, i, value):
+    def keep(ref, i, low_row, value):
         high, low = split(value)
         ref[i * 64:i * 64 + NL] = high
-        ref[256 + i * 64:256 + i * 64 + NL] = low
-
-    def both(result, i):
-        return result[i * 64:i * 64 + NL] + result[256 + i * 64:256 + i * 64 + NL]
-
-    def advance(f, carry):
-        @pl.when(f + AHEAD < NF)
-        def _():
-            send_halo(f + AHEAD)
-
-        @pl.when(has_left)
-        def _():
-            halo(f, 1).wait_recv()
-
-        @pl.when(has_right)
-        def _():
-            halo(f, 0).wait_recv()
-
-        turn = lax.rem(128 - f * NXC, 128)
-        below = pltpu.roll(yhalo[0, 0:LP], turn, axis=1)
-        above = pltpu.roll(yhalo[1, 0:LP], turn, axis=1)
-        lanes = lax.broadcasted_iota(jnp.int32, (LP, 128), 1)
-        for pair in range(NXC // 2):
-            for half in range(2):
-                x = 2 * pair + half
-                cells = [ms[f, x + 1, b] for b in range(NB)]
-                up = [pltpu.roll(c, 1, axis=1) for c in cells]
-                down = [pltpu.roll(c, 127, axis=1) for c in cells]
-                edge_low = below if x == 0 else pltpu.roll(below, 128 - x, axis=1)
-                edge_high = pltpu.roll(above, 127 - x, axis=1)
-                for b in range(NB):
-                    prev = jnp.where(lanes == 0, up[b - 1] if b else edge_low, up[b])
-                    after = jnp.where(lanes == 127, down[b + 1] if b < NB - 1 else edge_high, down[b])
-                    beside = ms[f, x, b] + ms[f, x + 2, b] + prev + after
-                    spread = cells[b] + kappa[x * NB + b] * (beside - 4.0 * cells[b])
-                    high, low = split(spread[0:NL])
-                    col = half * NYC + b * 128
-                    xs[pair, 0:NL, col:col + 128] = high
-                    xs[pair, 64:64 + NL, col:col + 128] = low
-                    xs[pair, 128:128 + NL, col:col + 128] = high
-            mixed = jnp.dot(mc[f], xs[pair], preferred_element_type=F32)
-            mx[f, 2 * pair] = mixed[0:LP, 0:NYC]
-            mx[f, 2 * pair + 1] = mixed[0:LP, NYC:]
-
+        ref[low_row + i * 64:low_row + i * 64 + NL] = low
+
+    def both(result, i, low_row):
+        return result[i * 64:i * 64 + NL] + result[low_row + i * 64:low_row + i * 64 + NL]
+
+    lanes = lax.broadcasted_iota(jnp.int32, (LP, 128), 1)
+
+    def stencil(f, x, pair, half, part, turn):
+        below, above = yhalo[part, 0], yhalo[part, 1]
+        cells = [ms[f, x + 1, b] for b in range(NB)]
+        up = [pltpu.roll(c, 1, axis=1) for c in cells]
+        down = [pltpu.roll(c, 127, axis=1) for c in cells]
+        edge_low = pltpu.roll(below, lax.rem(turn + 128 - x, 128), axis=1)
+        edge_high = pltpu.roll(above, lax.rem(turn + 127 - x, 128), axis=1)
+        for b in range(NB):
+            prev = jnp.where(lanes == 0, up[b - 1] if b else edge_low, up[b])
+            after = jnp.where(lanes == 127, down[b + 1] if b < NB - 1 else edge_high, down[b])
+            beside = ms[f, x, b] + ms[f, x + 2, b] + prev + after
+            spread = cells[b] + kappa[x * NB + b] * (beside - 4.0 * cells[b])
+            high, low = split(spread[0:NL])
+            col = half * NYC + b * 128
+            xs[pair, 0:NL, col:col + 128] = high
+            xs[pair, 64:64 + NL, col:col + 128] = low
+            xs[pair, 128:128 + NL, col:col + 128] = high
+
+    def blend(f, pair, x0, x1):
+        mixed = jnp.dot(mc[f], xs[pair], preferred_element_type=F32)
+        mx[f, x0] = mixed[0:LP, 0:NYC]
+        mx[f, x1] = mixed[0:LP, NYC:]
+
+    groups = ((1, 2), (0, 3))
+
+    def give_back(f, part):
         @pl.when(child)
         def _():
-            for i in range(4):
+            for n, i in enumerate(groups[part]):
                 total = mx[f, 3 * i, 0:NL] * nudge[3 * i:3 * i + 1, :]
                 for a in range(1, 3):
                     total = total + mx[f, 3 * i + a, 0:NL] * nudge[3 * i + a:3 * i + a + 1, :]
-                keep(lhs, i, total)
+                keep(lhs, n, 128, total)
 
         @pl.when(parent)
         def _():
-            for i in range(4):
-                keep(lhs, i, mx[f, nest_x[0] + i, 0:NL])
+            for n, i in enumerate(groups[part]):
+                keep(lhs, n, 128, mx[f, nest_x[0] + i, 0:NL])
 
         picked = jnp.dot(lhs[...], wsel[...], preferred_element_type=F32)
-        for i in range(4):
-            pay[f, i, 0:NL] = both(picked, i)
-        feedback(f).start()
+        for n in range(2):
+            pay[f, 2 * part + n, 0:NL] = both(picked, n, 128)
+        feedback(f, part).start()
+
+    def interior(f, carry):
+        @pl.when(f + AHEAD < NF)
+        def _():
+            send_halo(f + AHEAD)
+
+        @pl.when(f == 0)
+        def _():
+            await_columns(0)
+
+        @pl.when(f == 1)
+        def _():
+            await_columns(1)
+
+        part = jnp.minimum(f, 1)
+        turn = 128 - (f - part) * NXC
+        for pair in range(NXC // 2 - 1):
+            stencil(f, 2 * pair + 1, pair, 0, part, turn)
+            stencil(f, 2 * pair + 2, pair, 1, part, turn)
+            blend(f, pair, 2 * pair + 1, 2 * pair + 2)
+        give_back(f, 0)
 
         @pl.when(f == 0)
         def _():
@@ -339,18 +361,38 @@
 
         return carry
 
-    lax.fori_loop(0, NF, advance, 0)
+    lax.fori_loop(0, NF, interior, 0)
+
+    def border(f, carry):
+        @pl.when(has_left)
+        def _():
+            halo(f, 1).wait_recv()
+
+        @pl.when(has_right)
+        def _():
+            halo(f, 0).wait_recv()
+
+        part = jnp.minimum(f, 1)
+        turn = 128 - (f - part) * NXC
+        stencil(f, 0, NXC // 2 - 1, 0, part, turn)
+        stencil(f, NXC - 1, NXC // 2 - 1, 1, part, turn)
+        blend(f, NXC // 2 - 1, 0, NXC - 1)
+        give_back(f, 1)
+        return carry
+
+    lax.fori_loop(0, NF, border, 0)
 
     take = jnp.where(child, 1.0 / 9.0, 1.0)
     give = jnp.where(child, 0.0, 1.0)
 
     def finish(f, carry):
-        feedback(f).wait_recv()
+        for part in range(2):
+            feedback(f, part).wait_recv()
         for i in range(4):
-            keep(dlt, i, got[f, i, 0:NL] * take - pay[f, i, 0:NL] * give)
+            keep(dlt, i, 256, got[f, i, 0:NL] * take - pay[f, i, 0:NL] * give)
         laid = jnp.dot(dlt[...], wback[...], preferred_element_type=F32)
-        for i in range(4):
-            cu[i, 0:NL] = both(laid, i)
+        for n, i in enumerate(groups[0] + groups[1]):
+            cu[i, 0:NL] = both(laid, n, 256)
         for x in range(NXC):
             p = x - nest_x[0]
             index = jnp.where(child, x // 3, jnp.where((p >= 0) & (p < 4), p, 4))
@@ -392,14 +434,17 @@
 
     @pl.when(has_down)
     def _():
-        yedge(0).wait_send()
+        for part in range(2):
+            yedge(part, 0).wait_send()
 
     @pl.when(has_up)
     def _():
-        yedge(1).wait_send()
+        for part in range(2):
+            yedge(part, 1).wait_send()
 
     for f in range(NF):
-        feedback(f).wait_send()
+        for part in range(2):
+            feedback(f, part).wait_send()
         leave(f).wait()
     leave_obs.wait()
 
@@ -431,16 +476,14 @@
         value = turned[t * SLOTS:(t + 1) * SLOTS, z * 8 + y:z * 8 + y + 1]
         terms[s * SLOTS:(s + 1) * SLOTS, :] = jnp.where(lane == lanes[:, s:s + 1], value, 0.0)
 
-    def source(i, carry):
-        for u in range(4):
-            s = i * 4 + u
-            for k in range(SLOTS):
-                row = pl.ds(lax.shift_right_logical(index[k, s], 7), 1)
-                ref = add1 if k % 2 else add0
-                ref[row, :] = ref[row, :] + terms[pl.ds(s * SLOTS + k, 1), :]
+    def source(s, carry):
+        for k in range(SLOTS):
+            row = pl.ds(lax.shift_right_logical(index[k, s], 7), 1)
+            ref = add1 if k % 2 else add0
+            ref[row, :] = ref[row, :] + terms[pl.ds(s * SLOTS + k, 1), :]
         return carry
 
-    lax.fori_loop(0, NTY * NTX // 4, source, 0)
+    lax.fori_loop(0, NTY * NTX, source, 0)
     fetches[5].wait()
 
     def leave(f):
@@ -487,20 +530,20 @@
         pltpu.VMEM((NF, NXC, LP, NYC), F32),
         pltpu.VMEM((NYC, 128), BF16),
         pltpu.VMEM((128, NYC), BF16),
-        pltpu.VMEM((512, NYC), BF16),
+        pltpu.VMEM((256, NYC), BF16),
         pltpu.VMEM((NF, 4, LP, 128), F32),
         pltpu.VMEM((NF, 4, LP, 128), F32),
         pltpu.VMEM((512, 128), BF16),
         pltpu.VMEM((5, LP, NYC), F32),
-        pltpu.VMEM((2, LP, 128), F32),
-        pltpu.VMEM((2, LP, 128), F32),
+        pltpu.VMEM((2, 2, LP, 128), F32),
+        pltpu.VMEM((2, 2, LP, 128), F32),
         pltpu.VMEM((128, 128), F32),
         pltpu.VMEM((NTY, NTX, 128), F32),
         pltpu.VMEM((NTX, 128), F32),
         pltpu.VMEM((NTX, 128), F32),
         pltpu.VMEM((NZA, 8, 128), F32),
         pltpu.VMEM((NZA, 8, 128), F32),
-        DMA((NF,)), DMA((2, NF)), DMA((2, NF)), DMA((2,)), DMA((2,)), DMA((NF,)), DMA((NF,)),
+        DMA((NF,)), DMA((2, NF)), DMA((2, NF)), DMA((2, 2)), DMA((2, 2)), DMA((2, NF)), DMA((2, NF)),
         DMA((NTY - 1,)), DMA((NTY - 1,)), DMA((NYA - 1,)), DMA((NYA - 1,)), DMA((NZA - 1,)), DMA((NZA - 1,)),
         DMA((7,)), pltpu.SemaphoreType.REGULAR((3, 6)), DMA((NF + 1,)),
     ]

time: 40 us -> 42.8 us (1.070)
  the two profiles are of different devices: /device:TPU:25 before, /device:TPU:1 now
where the time goes in v3:
time: 42.8 us; the launch traced here: 42.7 us
  Pallas kernels  41.4 us (97%)
  between operations  1.3 us (3%)
    pallas_call x1, Pallas kernels, local(): pl.pallas_call(exchange_kernel, out_shape=(jax.ShapeDtypeStruct((NF, ROWS...  32.1 us
    pallas_call x1, Pallas kernels, local(): pl.pallas_call(scatter_kernel, out_shape=jax.ShapeDtypeStruct((total, 128...  9.3 us

profile of v3, /device:TPU:1, one launch (start us, length us, event | category | flops | bytes accessed | tf_op | source)
XLA Modules:
  0.0 42.7 jit_solution(10444825291154620889)
XLA Ops:
  1.3 32.1 %exchange.1 = (f32[5,1800,128]{2,1,0:T(8,128)}, f32[64,128]{1,0:T(8,128)}) custom-call(s32[1]{0:T(128)S(6)} %copy.13.nest_x_in, s32[1]{0:T(128)S(6)} %copy.14.nest_y_in, f32[5,1800,128]{2,1,0:T(8,128)} %bitcast.11, s32[36,1,128]{2,1,0:T(1,128)} %bitcast.14, f32[36,1,128]{2,1,0:T(1,128)} %bitcast.16, f32[12,384]{1,0:T(8,128)} %nudge_in.1, ...), custom_call_target="tpu_custom_call" | custom-call | tf_op jit(solution)/shard_map/exchange/pallas_call | solution.py:550
  33.4 9.3 %scatter.1 = f32[9000,128]{1,0:T(8,128)} custom-call(f32[64,128]{1,0:T(8,128)} %get-tuple-element.7.vals_in, s32[16,128]{1,0:T(8,128)} %bitcast.18, s32[1,128]{1,0:T(1,128)} %bitcast.19, f32[9000,128]{1,0:T(8,128)} %bitcast.12, s32[36,1,128]{2,1,0:T(1,128)} %bitcast.15), custom_call_target="tpu_custom_call" | custom-call | tf_op jit(solution)/shard_map/scatter/pallas_call | solution.py:565

commit v4 on v3

--- a/solution.py
+++ b/solution.py
@@ -31,7 +31,7 @@
     nest_x_in, nest_y_in, state, mask_in, kappa_in, nudge_in, mix_in, obs_in,
     out, obs_out,
     nest_x, nest_y, mask, kappa, nudge, mix, obs, packed,
-    raw, ms, xs, mc, mx, wsel, wback, lhs, pay, got, dlt, cu,
+    raw, ms, xs, xe, em, mc, mx, wsel, wback, lhs, pay, got, dlt, cu,
     ycols, yhalo, oa, ob, oc, od, oe, og,
     in_sem, hs_sem, hr_sem, ys_sem, yr_sem, gs_sem, gr_sem,
     os1, or1, os2, or2, os3, or3, small_sem, far_sem, out_sem,
@@ -111,10 +111,13 @@
         d = d - scale * lax.broadcasted_iota(jnp.int32, shape, 1 - ydim) - off
         return jnp.where((d >= 0) & (d < scale), 1.0, 0.0).astype(BF16)
 
-    wsel[...] = selection((NYC, 128), 0)
-    wback[...] = selection((128, NYC), 1)
+    wsel[0:NYC] = selection((NYC, 128), 0)
+    wsel[NYC:] = wsel[0:NYC]
+    wback[0:128] = selection((128, NYC), 1)
+    wback[128:] = wback[0:128]
     mc[...] = jnp.zeros_like(mc)
     xs[...] = jnp.zeros_like(xs)
+    xe[...] = jnp.zeros_like(xe)
     for f in range(NF):
         high, low = split(mix[f, :, 0, :])
         mc[f, 0:NL, 0:NL] = high
@@ -134,13 +137,11 @@
 
     @pl.when(ty == 0)
     def _():
-        for part in range(2):
-            yhalo[part, 0] = jnp.zeros(yhalo.shape[2:], F32)
+        yhalo[0] = jnp.zeros(yhalo.shape[1:], F32)
 
     @pl.when(ty == NTY - 1)
     def _():
-        for part in range(2):
-            yhalo[part, 1] = jnp.zeros(yhalo.shape[2:], F32)
+        yhalo[1] = jnp.zeros(yhalo.shape[1:], F32)
 
     def obs1(d):
         peer = (ty + d) % NTY
@@ -180,77 +181,50 @@
         def _():
             halo(f, 1).start()
 
-    def plane(f, x):
-        for b in range(NB):
-            r = x * NB + b
-            ms[f, x + 1, b, 0:NL] = raw[f, pl.ds(r, NL, stride=STEP), :] * mask[r].astype(F32)
-
-    def columns(f, shift, first, last):
+    def ends(first, last, row, x):
+        pair = jnp.where(row < 64, first, last)
+        return pltpu.roll(pair, 2 * x, axis=1) if x else pair
+
+    def planes(f, carry):
+        fetch(f).wait()
+        edge = jnp.zeros((NL, 128), F32)
         for x in range(NXC):
-            here = lane == shift + x
-            first = jnp.where(here, ms[f, x + 1, 0, 0:NL, 0:1], first)
-            last = jnp.where(here, ms[f, x + 1, NB - 1, 0:NL, 127:128], last)
-        return first, last
-
-    def yedge(part, side):
+            value = []
+            for b in range(NB):
+                r = x * NB + b
+                value.append(raw[f, pl.ds(r, NL, stride=STEP), :] * mask[r].astype(F32))
+                ms[f, x + 1, b, 0:NL] = value[b]
+            here = (lane == 2 * x) | (lane == (2 * x - 1) % 128)
+            edge = jnp.where(here, ends(value[0], value[NB - 1], lane, x), edge)
+        turned = pltpu.roll(edge, 2 * NXC * f, axis=1)
+        return jnp.where(((lane + 1 - 2 * NXC * f) & 127) < 2 * NXC, turned, carry)
+
+    ycols[0:NL] = lax.fori_loop(0, NF, planes, jnp.zeros((NL, 128), F32))
+
+    def yedge(side):
         return pltpu.make_async_remote_copy(
-            ycols.at[part, side, pl.ds(0, NL)], yhalo.at[part, 1 - side, pl.ds(0, NL)],
-            ys_sem.at[part, side], yr_sem.at[part, side],
+            ycols.at[pl.ds(0, NL)], yhalo.at[1 - side, pl.ds(0, NL)], ys_sem.at[side], yr_sem.at[side],
             device_id=dev(y=ty - 1 if side == 0 else ty + 1), device_id_type=MESH,
         )
 
-    def send_columns(part, first, last):
-        ycols[part, 0, 0:NL] = first
-        ycols[part, 1, 0:NL] = last
-
-        @pl.when(has_down)
-        def _():
-            yedge(part, 0).start()
-
-        @pl.when(has_up)
-        def _():
-            yedge(part, 1).start()
-
-    def await_columns(part):
-        @pl.when(has_down)
-        def _():
-            yedge(part, 1).wait_recv()
-
-        @pl.when(has_up)
-        def _():
-            yedge(part, 0).wait_recv()
-
-    zero = jnp.zeros((NL, 128), F32)
-    fetch(0).wait()
-    for x in (0, NXC - 1, *range(1, NXC - 1)):
-        plane(0, x)
-    first, last = columns(0, 0, zero, zero)
     pl.semaphore_wait(barrier, 1 + len(ring) + jnp.where(wrap_left | wrap_right, 1, 0))
-    send_columns(0, first, last)
-    send_halo(0)
+
+    @pl.when(has_down)
+    def _():
+        yedge(0).start()
+
+    @pl.when(has_up)
+    def _():
+        yedge(1).start()
+
+    for f in range(AHEAD):
+        send_halo(f)
     vouch(0, range(6))
-
-    def planes(f, carry):
-        first, last = carry
-        fetch(f).wait()
-        plane(f, 0)
-        plane(f, NXC - 1)
-
-        @pl.when(f < AHEAD)
-        def _():
-            send_halo(f)
-
-        for x in range(1, NXC - 1):
-            plane(f, x)
-        return columns(f, (f - 1) * NXC, first, last)
-
-    first, last = lax.fori_loop(1, NF, planes, (zero, zero))
-    send_columns(1, first, last)
-
-    vouched(0, range(6))
-    vouch(1, (4, 5))
-    for d in range(1, NTY):
-        obs1(d).start()
+    row = lax.broadcasted_iota(jnp.int32, (1, 128), 1)
+    kends = jnp.zeros((1, 128), F32)
+    for x in range(NXC):
+        here = (row == 2 * x) | (row == (2 * x - 1) % 128)
+        kends = jnp.where(here, ends(kappa[x * NB], kappa[x * NB + NB - 1], row, x), kends)
 
     def feedback(f, part):
         planes = pl.ds(2 * part, 2)
@@ -260,33 +234,51 @@
             device_id=dev(g=1 - grp), device_id_type=MESH,
         )
 
-    def keep(ref, i, low_row, value):
+    def keep(ref, i, value):
         high, low = split(value)
-        ref[i * 64:i * 64 + NL] = high
-        ref[low_row + i * 64:low_row + i * 64 + NL] = low
-
-    def both(result, i, low_row):
-        return result[i * 64:i * 64 + NL] + result[low_row + i * 64:low_row + i * 64 + NL]
-
-    lanes = lax.broadcasted_iota(jnp.int32, (LP, 128), 1)
-
-    def stencil(f, x, pair, half, part, turn):
-        below, above = yhalo[part, 0], yhalo[part, 1]
-        cells = [ms[f, x + 1, b] for b in range(NB)]
-        up = [pltpu.roll(c, 1, axis=1) for c in cells]
-        down = [pltpu.roll(c, 127, axis=1) for c in cells]
-        edge_low = pltpu.roll(below, lax.rem(turn + 128 - x, 128), axis=1)
-        edge_high = pltpu.roll(above, lax.rem(turn + 127 - x, 128), axis=1)
-        for b in range(NB):
-            prev = jnp.where(lanes == 0, up[b - 1] if b else edge_low, up[b])
-            after = jnp.where(lanes == 127, down[b + 1] if b < NB - 1 else edge_high, down[b])
-            beside = ms[f, x, b] + ms[f, x + 2, b] + prev + after
-            spread = cells[b] + kappa[x * NB + b] * (beside - 4.0 * cells[b])
-            high, low = split(spread[0:NL])
-            col = half * NYC + b * 128
-            xs[pair, 0:NL, col:col + 128] = high
-            xs[pair, 64:64 + NL, col:col + 128] = low
-            xs[pair, 128:128 + NL, col:col + 128] = high
+        width = value.shape[1]
+        ref[i * 64:i * 64 + NL, 0:width] = high
+        ref[i * 64:i * 64 + NL, width:2 * width] = low
+
+    def fill(ref, start, stop, columns, value):
+        high, low = split(value)
+        n = stop - start
+        ref[start:stop, columns] = high[0:n]
+        ref[64 + start:64 + stop, columns] = low[0:n]
+        ref[128 + start:128 + stop, columns] = high[0:n]
+
+    lane16 = lax.broadcasted_iota(jnp.int32, (16, 128), 1)
+
+    def stencil(f, xpair, pair):
+        for start, size in ((0, 16), (16, 16), (32, 16), (48, 8)):
+            rows = slice(start, start + size)
+            lanes = lane16[0:size]
+            for half, x in enumerate(xpair):
+                cells = [ms[f, x + 1, b, rows] for b in range(NB)]
+                up = [pltpu.roll(c, 1, axis=1) for c in cells]
+                down = [pltpu.roll(c, 127, axis=1) for c in cells]
+                for b in range(NB):
+                    prev = jnp.where(lanes == 0, up[b - 1] if b else 0.0, up[b])
+                    after = jnp.where(lanes == 127, down[b + 1] if b < NB - 1 else 0.0, down[b])
+                    beside = ms[f, x, b, rows] + ms[f, x + 2, b, rows] + prev + after
+                    spread = cells[b] + kappa[x * NB + b] * (beside - 4.0 * cells[b])
+                    col = half * NYC + b * 128
+                    fill(xs.at[pair], start, min(start + size, NL), slice(col, col + 128), spread)
+
+    def mix_ends(f):
+        even = (lane & 1) == 0
+        outer = jnp.where(
+            even, pltpu.roll(yhalo[0, 0:NL], 1, axis=1), pltpu.roll(yhalo[1, 0:NL], 127, axis=1)
+        )
+        outer = pltpu.roll(outer, lax.rem(256 - 2 * NXC * f, 128), axis=1) * kends
+        fill(xe, 0, NL, slice(0, 128), outer)
+        em[f] = jnp.dot(mc[f], xe[...], preferred_element_type=F32)[0:LP]
+
+    def add_ends(f, x):
+        term = em[f, 0:NL]
+        term = pltpu.roll(term, 128 - 2 * x, axis=1) if x else term
+        mx[f, x, 0:NL, 0:128] += jnp.where(lane == 0, term, 0.0)
+        mx[f, x, 0:NL, NYC - 128:] += jnp.where(lane == 127, term, 0.0)
 
     def blend(f, pair, x0, x1):
         mixed = jnp.dot(mc[f], xs[pair], preferred_element_type=F32)
@@ -302,40 +294,73 @@
                 total = mx[f, 3 * i, 0:NL] * nudge[3 * i:3 * i + 1, :]
                 for a in range(1, 3):
                     total = total + mx[f, 3 * i + a, 0:NL] * nudge[3 * i + a:3 * i + a + 1, :]
-                keep(lhs, n, 128, total)
+                keep(lhs, n, total)
 
         @pl.when(parent)
         def _():
             for n, i in enumerate(groups[part]):
-                keep(lhs, n, 128, mx[f, nest_x[0] + i, 0:NL])
+                keep(lhs, n, mx[f, nest_x[0] + i, 0:NL])
 
         picked = jnp.dot(lhs[...], wsel[...], preferred_element_type=F32)
         for n in range(2):
-            pay[f, 2 * part + n, 0:NL] = both(picked, n, 128)
+            pay[f, 2 * part + n, 0:NL] = picked[n * 64:n * 64 + NL]
         feedback(f, part).start()
+
+    def ready(f):
+        mix_ends(f)
+        for x in range(1, NXC - 1):
+            add_ends(f, x)
+        give_back(f, 0)
 
     def interior(f, carry):
         @pl.when(f + AHEAD < NF)
         def _():
             send_halo(f + AHEAD)
 
-        @pl.when(f == 0)
-        def _():
-            await_columns(0)
+        for pair in range(NXC // 2 - 1):
+            stencil(f, (2 * pair + 1, 2 * pair + 2), pair)
+            blend(f, pair, 2 * pair + 1, 2 * pair + 2)
 
         @pl.when(f == 1)
         def _():
-            await_columns(1)
-
-        part = jnp.minimum(f, 1)
-        turn = 128 - (f - part) * NXC
-        for pair in range(NXC // 2 - 1):
-            stencil(f, 2 * pair + 1, pair, 0, part, turn)
-            stencil(f, 2 * pair + 2, pair, 1, part, turn)
-            blend(f, pair, 2 * pair + 1, 2 * pair + 2)
-        give_back(f, 0)
-
-        @pl.when(f == 0)
+            @pl.when(has_down)
+            def _():
+                yedge(1).wait_recv()
+
+            @pl.when(has_up)
+            def _():
+                yedge(0).wait_recv()
+
+        @pl.when(f > 0)
+        def _():
+            ready(f - 1)
+
+        return carry
+
+    lax.fori_loop(0, NF, interior, 0)
+    ready(NF - 1)
+
+    vouched(0, range(6))
+    vouch(1, (4, 5))
+    for d in range(1, NTY):
+        obs1(d).start()
+
+    def border(f, carry):
+        @pl.when(has_left)
+        def _():
+            halo(f, 1).wait_recv()
+
+        @pl.when(has_right)
+        def _():
+            halo(f, 0).wait_recv()
+
+        stencil(f, (0, NXC - 1), NXC // 2 - 1)
+        blend(f, NXC // 2 - 1, 0, NXC - 1)
+        add_ends(f, 0)
+        add_ends(f, NXC - 1)
+        give_back(f, 1)
+
+        @pl.when(f == 1)
         def _():
             vouched(1, (4, 5))
             vouch(2, (4, 5))
@@ -347,7 +372,7 @@
             for d in range(1, NYA):
                 obs2(d).start()
 
-        @pl.when(f == 2)
+        @pl.when(f == 3)
         def _():
             vouched(2, (4, 5))
             for d in range(1, NYA):
@@ -361,25 +386,6 @@
 
         return carry
 
-    lax.fori_loop(0, NF, interior, 0)
-
-    def border(f, carry):
-        @pl.when(has_left)
-        def _():
-            halo(f, 1).wait_recv()
-
-        @pl.when(has_right)
-        def _():
-            halo(f, 0).wait_recv()
-
-        part = jnp.minimum(f, 1)
-        turn = 128 - (f - part) * NXC
-        stencil(f, 0, NXC // 2 - 1, 0, part, turn)
-        stencil(f, NXC - 1, NXC // 2 - 1, 1, part, turn)
-        blend(f, NXC // 2 - 1, 0, NXC - 1)
-        give_back(f, 1)
-        return carry
-
     lax.fori_loop(0, NF, border, 0)
 
     take = jnp.where(child, 1.0 / 9.0, 1.0)
@@ -389,10 +395,10 @@
         for part in range(2):
             feedback(f, part).wait_recv()
         for i in range(4):
-            keep(dlt, i, 256, got[f, i, 0:NL] * take - pay[f, i, 0:NL] * give)
+            keep(dlt, i, got[f, i, 0:NL] * take - pay[f, i, 0:NL] * give)
         laid = jnp.dot(dlt[...], wback[...], preferred_element_type=F32)
         for n, i in enumerate(groups[0] + groups[1]):
-            cu[i, 0:NL] = both(laid, n, 256)
+            cu[i, 0:NL] = laid[n * 64:n * 64 + NL]
         for x in range(NXC):
             p = x - nest_x[0]
             index = jnp.where(child, x // 3, jnp.where((p >= 0) & (p < 4), p, 4))
@@ -434,13 +440,11 @@
 
     @pl.when(has_down)
     def _():
-        for part in range(2):
-            yedge(part, 0).wait_send()
+        yedge(0).wait_send()
 
     @pl.when(has_up)
     def _():
-        for part in range(2):
-            yedge(part, 1).wait_send()
+        yedge(1).wait_send()
 
     for f in range(NF):
         for part in range(2):
@@ -526,24 +530,26 @@
         pltpu.VMEM((NF, ROWS, 128), F32),
         pltpu.VMEM((NF, NXC + 2, NB, LP, 128), F32),
         pltpu.VMEM((NXC // 2, 192, 2 * NYC), BF16),
+        pltpu.VMEM((192, 128), BF16),
+        pltpu.VMEM((NF, LP, 128), F32),
         pltpu.VMEM((NF, 64, 192), BF16),
         pltpu.VMEM((NF, NXC, LP, NYC), F32),
-        pltpu.VMEM((NYC, 128), BF16),
-        pltpu.VMEM((128, NYC), BF16),
+        pltpu.VMEM((2 * NYC, 128), BF16),
         pltpu.VMEM((256, NYC), BF16),
+        pltpu.VMEM((128, 2 * NYC), BF16),
         pltpu.VMEM((NF, 4, LP, 128), F32),
         pltpu.VMEM((NF, 4, LP, 128), F32),
-        pltpu.VMEM((512, 128), BF16),
+        pltpu.VMEM((256, 256), BF16),
         pltpu.VMEM((5, LP, NYC), F32),
-        pltpu.VMEM((2, 2, LP, 128), F32),
-        pltpu.VMEM((2, 2, LP, 128), F32),
+        pltpu.VMEM((LP, 128), F32),
+        pltpu.VMEM((2, LP, 128), F32),
         pltpu.VMEM((128, 128), F32),
         pltpu.VMEM((NTY, NTX, 128), F32),
         pltpu.VMEM((NTX, 128), F32),
         pltpu.VMEM((NTX, 128), F32),
         pltpu.VMEM((NZA, 8, 128), F32),
         pltpu.VMEM((NZA, 8, 128), F32),
-        DMA((NF,)), DMA((2, NF)), DMA((2, NF)), DMA((2, 2)), DMA((2, 2)), DMA((2, NF)), DMA((2, NF)),
+        DMA((NF,)), DMA((2, NF)), DMA((2, NF)), DMA((2,)), DMA((2,)), DMA((2, NF)), DMA((2, NF)),
         DMA((NTY - 1,)), DMA((NTY - 1,)), DMA((NYA - 1,)), DMA((NYA - 1,)), DMA((NZA - 1,)), DMA((NZA - 1,)),
         DMA((7,)), pltpu.SemaphoreType.REGULAR((3, 6)), DMA((NF + 1,)),
     ]

time: 42.8 us -> 44.6 us (1.042)
  the two profiles are of different devices: /device:TPU:1 before, /device:TPU:6 now
where the time goes in v4:
time: 44.6 us; the launch traced here: 44.5 us
  Pallas kernels  43.2 us (97%)
  between operations  1.3 us (3%)
    pallas_call x1, Pallas kernels, local(): pl.pallas_call(exchange_kernel, out_shape=(jax.ShapeDtypeStruct((NF, ROWS...  33.9 us
    pallas_call x1, Pallas kernels, local(): pl.pallas_call(scatter_kernel, out_shape=jax.ShapeDtypeStruct((total, 128...  9.3 us

profile of v4, /device:TPU:6, one launch (start us, length us, event | category | flops | bytes accessed | tf_op | source)
XLA Modules:
  0.0 44.5 jit_solution(2730915842555690141)
XLA Ops:
  1.3 33.9 %exchange.1 = (f32[5,1800,128]{2,1,0:T(8,128)}, f32[64,128]{1,0:T(8,128)}) custom-call(s32[1]{0:T(128)S(6)} %copy.13.nest_x_in, s32[1]{0:T(128)S(6)} %copy.14.nest_y_in, f32[5,1800,128]{2,1,0:T(8,128)} %bitcast.11, s32[36,1,128]{2,1,0:T(1,128)} %bitcast.14, f32[36,1,128]{2,1,0:T(1,128)} %bitcast.16, f32[12,384]{1,0:T(8,128)} %nudge_in.1, ...), custom_call_target="tpu_custom_call" | custom-call | tf_op jit(solution)/shard_map/exchange/pallas_call | solution.py:556
  35.2 9.3 %scatter.1 = f32[9000,128]{1,0:T(8,128)} custom-call(f32[64,128]{1,0:T(8,128)} %get-tuple-element.7.vals_in, s32[16,128]{1,0:T(8,128)} %bitcast.18, s32[1,128]{1,0:T(1,128)} %bitcast.19, f32[9000,128]{1,0:T(8,128)} %bitcast.12, s32[36,1,128]{2,1,0:T(1,128)} %bitcast.15), custom_call_target="tpu_custom_call" | custom-call | tf_op jit(solution)/shard_map/scatter/pallas_call | solution.py:571

commit v5 on v2

--- a/solution.py
+++ b/solution.py
@@ -32,7 +32,7 @@
     out, obs_out,
     nest_x, nest_y, mask, kappa, nudge, mix, obs, packed,
     raw, ms, xs, mc, mx, wsel, wback, lhs, pay, got, dlt, cu,
-    ycols, yhalo, oa, ob, oc, od, oe, og,
+    ycols, yhalo, outer, oa, ob, oc, od, oe, og,
     in_sem, hs_sem, hr_sem, ys_sem, yr_sem, gs_sem, gr_sem,
     os1, or1, os2, or2, os3, or3, small_sem, far_sem, out_sem,
 ):
@@ -111,8 +111,10 @@
         d = d - scale * lax.broadcasted_iota(jnp.int32, shape, 1 - ydim) - off
         return jnp.where((d >= 0) & (d < scale), 1.0, 0.0).astype(BF16)
 
-    wsel[...] = selection((NYC, 128), 0)
-    wback[...] = selection((128, NYC), 1)
+    wsel[0:NYC] = selection((NYC, 128), 0)
+    wsel[NYC:] = wsel[0:NYC]
+    wback[0:128] = selection((128, NYC), 1)
+    wback[128:] = wback[0:128]
     mc[...] = jnp.zeros_like(mc)
     xs[...] = jnp.zeros_like(xs)
     for f in range(NF):
@@ -121,7 +123,6 @@
         mc[f, 0:NL, 64:64 + NL] = high
         mc[f, 0:NL, 128:128 + NL] = low
     cu[4] = jnp.zeros(cu.shape[1:], F32)
-    ycols[...] = jnp.zeros_like(ycols)
 
     @pl.when(tx == 0)
     def _():
@@ -140,9 +141,6 @@
     @pl.when(ty == NTY - 1)
     def _():
         yhalo[1] = jnp.zeros(yhalo.shape[1:], F32)
-
-    pl.semaphore_wait(barrier, 1 + len(ring) + jnp.where(wrap_left | wrap_right, 1, 0))
-    vouch(0, range(6))
 
     def obs1(d):
         peer = (ty + d) % NTY
@@ -182,44 +180,47 @@
         def _():
             halo(f, 1).start()
 
-    def plane(f, x):
-        for b in range(NB):
-            r = x * NB + b
-            ms[f, x + 1, b, 0:NL] = raw[f, pl.ds(r, NL, stride=STEP), :] * mask[r].astype(F32)
-
-    def edges(f, carry):
+    def meet():
+        pl.semaphore_wait(barrier, 1 + len(ring) + jnp.where(wrap_left | wrap_right, 1, 0))
+        vouch(0, range(6))
+
+    @pl.when(za != 0)
+    def _():
+        meet()
+
+    def planes(f, carry):
         fetch(f).wait()
-        plane(f, 0)
-        plane(f, NXC - 1)
-
-        @pl.when(f < AHEAD)
+        edge = jnp.zeros((NL, 128), F32)
+        for x in range(NXC):
+            value = []
+            for b in range(NB):
+                r = x * NB + b
+                value.append(raw[f, pl.ds(r, NL, stride=STEP), :] * mask[r].astype(F32))
+                ms[f, x + 1, b, 0:NL] = value[b]
+            pair = jnp.where(lane < 64, value[0], value[NB - 1])
+            here = (lane == 2 * x) | (lane == (2 * x - 1) % 128)
+            edge = jnp.where(here, pltpu.roll(pair, 2 * x, axis=1) if x else pair, edge)
+
+        @pl.when((f < AHEAD) & (za != 0))
         def _():
             send_halo(f)
 
-        return carry
-
-    lax.fori_loop(0, NF, edges, 0)
-
-    def planes(f, carry):
-        first, last = carry
-        for x in range(1, NXC - 1):
-            plane(f, x)
-        for x in range(NXC):
-            here = lane == f * NXC + x
-            first = jnp.where(here, ms[f, x + 1, 0, 0:NL, 0:1], first)
-            last = jnp.where(here, ms[f, x + 1, NB - 1, 0:NL, 127:128], last)
-        return first, last
-
-    zero = jnp.zeros((NL, 128), F32)
-    first, last = lax.fori_loop(0, NF, planes, (zero, zero))
-    ycols[0, 0:NL] = first
-    ycols[1, 0:NL] = last
+        turned = pltpu.roll(edge, 2 * NXC * f, axis=1)
+        return jnp.where(((lane + 1 - 2 * NXC * f) & 127) < 2 * NXC, turned, carry)
+
+    ycols[0:NL] = lax.fori_loop(0, NF, planes, jnp.zeros((NL, 128), F32))
 
     def yedge(side):
         return pltpu.make_async_remote_copy(
-            ycols.at[side, pl.ds(0, NL)], yhalo.at[1 - side, pl.ds(0, NL)], ys_sem.at[side], yr_sem.at[side],
+            ycols.at[pl.ds(0, NL)], yhalo.at[1 - side, pl.ds(0, NL)], ys_sem.at[side], yr_sem.at[side],
             device_id=dev(y=ty - 1 if side == 0 else ty + 1), device_id_type=MESH,
         )
+
+    @pl.when(za == 0)
+    def _():
+        meet()
+        for f in range(AHEAD):
+            send_halo(f)
 
     @pl.when(has_down)
     def _():
@@ -242,6 +243,11 @@
     def _():
         yedge(0).wait_recv()
 
+    even = (lane & 1) == 0
+    outer[0:NL] = jnp.where(
+        even, pltpu.roll(yhalo[0, 0:NL], 1, axis=1), pltpu.roll(yhalo[1, 0:NL], 127, axis=1)
+    )
+
     def feedback(f):
         return pltpu.make_async_remote_copy(
             pay.at[f, :, pl.ds(0, NL)], got.at[f, :, pl.ds(0, NL)], gs_sem.at[f], gr_sem.at[f],
@@ -250,11 +256,33 @@
 
     def keep(ref, i, value):
         high, low = split(value)
-        ref[i * 64:i * 64 + NL] = high
-        ref[256 + i * 64:256 + i * 64 + NL] = low
-
-    def both(result, i):
-        return result[i * 64:i * 64 + NL] + result[256 + i * 64:256 + i * 64 + NL]
+        width = value.shape[1]
+        ref[i * 64:i * 64 + NL, 0:width] = high
+        ref[i * 64:i * 64 + NL, width:2 * width] = low
+
+    lane16 = lax.broadcasted_iota(jnp.int32, (16, 128), 1)
+
+    def stencil(f, pair, local):
+        for start, size in ((0, 16), (16, 16), (32, 16), (48, 8)):
+            rows = slice(start, start + size)
+            keep_rows = min(size, NL - start)
+            lanes = lane16[0:size]
+            for half in range(2):
+                x = 2 * pair + half
+                cells = [ms[f, x + 1, b, rows] for b in range(NB)]
+                edge = pltpu.roll(local[rows], 128 - 2 * x, axis=1) if x else local[rows]
+                up = [pltpu.roll(c, 1, axis=1) for c in cells]
+                down = [pltpu.roll(c, 127, axis=1) for c in cells]
+                for b in range(NB):
+                    prev = jnp.where(lanes == 0, up[b - 1] if b else edge, up[b])
+                    after = jnp.where(lanes == 127, down[b + 1] if b < NB - 1 else edge, down[b])
+                    beside = ms[f, x, b, rows] + ms[f, x + 2, b, rows] + prev + after
+                    spread = cells[b] + kappa[x * NB + b] * (beside - 4.0 * cells[b])
+                    high, low = split(spread)
+                    columns = slice(half * NYC + b * 128, half * NYC + b * 128 + 128)
+                    xs[pair, start:start + keep_rows, columns] = high[0:keep_rows]
+                    xs[pair, 64 + start:64 + start + keep_rows, columns] = low[0:keep_rows]
+                    xs[pair, 128 + start:128 + start + keep_rows, columns] = high[0:keep_rows]
 
     def advance(f, carry):
         @pl.when(f + AHEAD < NF)
@@ -269,28 +297,9 @@
         def _():
             halo(f, 0).wait_recv()
 
-        turn = lax.rem(128 - f * NXC, 128)
-        below = pltpu.roll(yhalo[0, 0:LP], turn, axis=1)
-        above = pltpu.roll(yhalo[1, 0:LP], turn, axis=1)
-        lanes = lax.broadcasted_iota(jnp.int32, (LP, 128), 1)
+        local = pltpu.roll(outer[...], lax.rem(256 - 2 * NXC * f, 128), axis=1)
         for pair in range(NXC // 2):
-            for half in range(2):
-                x = 2 * pair + half
-                cells = [ms[f, x + 1, b] for b in range(NB)]
-                up = [pltpu.roll(c, 1, axis=1) for c in cells]
-                down = [pltpu.roll(c, 127, axis=1) for c in cells]
-                edge_low = below if x == 0 else pltpu.roll(below, 128 - x, axis=1)
-                edge_high = pltpu.roll(above, 127 - x, axis=1)
-                for b in range(NB):
-                    prev = jnp.where(lanes == 0, up[b - 1] if b else edge_low, up[b])
-                    after = jnp.where(lanes == 127, down[b + 1] if b < NB - 1 else edge_high, down[b])
-                    beside = ms[f, x, b] + ms[f, x + 2, b] + prev + after
-                    spread = cells[b] + kappa[x * NB + b] * (beside - 4.0 * cells[b])
-                    high, low = split(spread[0:NL])
-                    col = half * NYC + b * 128
-                    xs[pair, 0:NL, col:col + 128] = high
-                    xs[pair, 64:64 + NL, col:col + 128] = low
-                    xs[pair, 128:128 + NL, col:col + 128] = high
+            stencil(f, pair, local)
             mixed = jnp.dot(mc[f], xs[pair], preferred_element_type=F32)
             mx[f, 2 * pair] = mixed[0:LP, 0:NYC]
             mx[f, 2 * pair + 1] = mixed[0:LP, NYC:]
@@ -310,7 +319,7 @@
 
         picked = jnp.dot(lhs[...], wsel[...], preferred_element_type=F32)
         for i in range(4):
-            pay[f, i, 0:NL] = both(picked, i)
+            pay[f, i, 0:NL] = picked[i * 64:i * 64 + NL]
         feedback(f).start()
 
         @pl.when(f == 0)
@@ -350,7 +359,7 @@
             keep(dlt, i, got[f, i, 0:NL] * take - pay[f, i, 0:NL] * give)
         laid = jnp.dot(dlt[...], wback[...], preferred_element_type=F32)
         for i in range(4):
-            cu[i, 0:NL] = both(laid, i)
+            cu[i, 0:NL] = laid[i * 64:i * 64 + NL]
         for x in range(NXC):
             p = x - nest_x[0]
             index = jnp.where(child, x // 3, jnp.where((p >= 0) & (p < 4), p, 4))
@@ -485,15 +494,16 @@
         pltpu.VMEM((NXC // 2, 192, 2 * NYC), BF16),
         pltpu.VMEM((NF, 64, 192), BF16),
         pltpu.VMEM((NF, NXC, LP, NYC), F32),
-        pltpu.VMEM((NYC, 128), BF16),
-        pltpu.VMEM((128, NYC), BF16),
-        pltpu.VMEM((512, NYC), BF16),
+        pltpu.VMEM((2 * NYC, 128), BF16),
+        pltpu.VMEM((256, NYC), BF16),
+        pltpu.VMEM((256, 2 * NYC), BF16),
         pltpu.VMEM((NF, 4, LP, 128), F32),
         pltpu.VMEM((NF, 4, LP, 128), F32),
-        pltpu.VMEM((512, 128), BF16),
+        pltpu.VMEM((256, 256), BF16),
         pltpu.VMEM((5, LP, NYC), F32),
+        pltpu.VMEM((LP, 128), F32),
         pltpu.VMEM((2, LP, 128), F32),
-        pltpu.VMEM((2, LP, 128), F32),
+        pltpu.VMEM((LP, 128), F32),
         pltpu.VMEM((128, 128), F32),
         pltpu.VMEM((NTY, NTX, 128), F32),
         pltpu.VMEM((NTX, 128), F32),

time: 40 us -> 39.6 us (0.990)
  Pallas kernels: 38.6 us -> 38.1 us
    pallas_call x1, Pallas kernels: 29.3 us -> 28.9 us  [local(): pl.pallas_call(exchange_kernel, out_shape=(jax.ShapeDtypeStruct((NF, ROWS...]
where the time goes in v5:
time: 39.6 us; the launch traced here: 39.4 us
  Pallas kernels  38.1 us (96%)
  between operations  1.3 us (3%)
    pallas_call x1, Pallas kernels, local(): pl.pallas_call(exchange_kernel, out_shape=(jax.ShapeDtypeStruct((NF, ROWS...  28.9 us
    pallas_call x1, Pallas kernels, local(): pl.pallas_call(scatter_kernel, out_shape=jax.ShapeDtypeStruct((total, 128...  9.26 us

profile of v5, /device:TPU:25, one launch (start us, length us, event | category | flops | bytes accessed | tf_op | source)
XLA Modules:
  0.0 39.4 jit_solution(17480624428025299632)
XLA Ops:
  1.3 28.9 %exchange.1 = (f32[5,1800,128]{2,1,0:T(8,128)}, f32[64,128]{1,0:T(8,128)}) custom-call(s32[1]{0:T(128)S(6)} %copy.13.nest_x_in, s32[1]{0:T(128)S(6)} %copy.14.nest_y_in, f32[5,1800,128]{2,1,0:T(8,128)} %bitcast.11, s32[36,1,128]{2,1,0:T(1,128)} %bitcast.14, f32[36,1,128]{2,1,0:T(1,128)} %bitcast.16, f32[12,384]{1,0:T(8,128)} %nudge_in.1, ...), custom_call_target="tpu_custom_call" | custom-call | tf_op jit(solution)/shard_map/exchange/pallas_call | solution.py:517
  30.2 9.3 %scatter.1 = f32[9000,128]{1,0:T(8,128)} custom-call(f32[64,128]{1,0:T(8,128)} %get-tuple-element.7.vals_in, s32[16,128]{1,0:T(8,128)} %bitcast.18, s32[1,128]{1,0:T(1,128)} %bitcast.19, f32[9000,128]{1,0:T(8,128)} %bitcast.12, s32[36,1,128]{2,1,0:T(1,128)} %bitcast.15), custom_call_target="tpu_custom_call" | custom-call | tf_op jit(solution)/shard_map/scatter/pallas_call | solution.py:532

commit v6 on v5

--- a/solution.py
+++ b/solution.py
@@ -17,7 +17,7 @@
 STEP = NXC * NB
 NTY, NTX, NYA, NZA = 4, 32, 4, 8
 SLOTS = 16
-AHEAD = 2
+AHEAD = 3
 VMEM_BYTES = 63 * 2**20
 
 
@@ -172,13 +172,13 @@
         )
 
     def send_halo(f):
+        @pl.when(has_right)
+        def _():
+            halo(f, 1).start()
+
         @pl.when(has_left)
         def _():
             halo(f, 0).start()
-
-        @pl.when(has_right)
-        def _():
-            halo(f, 1).start()
 
     def meet():
         pl.semaphore_wait(barrier, 1 + len(ring) + jnp.where(wrap_left | wrap_right, 1, 0))

time: 39.6 us -> 40.2 us (1.015)
  the two profiles are of different devices: /device:TPU:25 before, /device:TPU:4 now
where the time goes in v6:
time: 40.2 us; the launch traced here: 40 us
  Pallas kernels  38.7 us (96%)
  between operations  1.3 us (3%)
    pallas_call x1, Pallas kernels, local(): pl.pallas_call(exchange_kernel, out_shape=(jax.ShapeDtypeStruct((NF, ROWS...  29.5 us
    pallas_call x1, Pallas kernels, local(): pl.pallas_call(scatter_kernel, out_shape=jax.ShapeDtypeStruct((total, 128...  9.26 us

profile of v6, /device:TPU:4, one launch (start us, length us, event | category | flops | bytes accessed | tf_op | source)
XLA Modules:
  0.0 40.0 jit_solution(9508124604154577058)
XLA Ops:
  1.3 29.5 %exchange.1 = (f32[5,1800,128]{2,1,0:T(8,128)}, f32[64,128]{1,0:T(8,128)}) custom-call(s32[1]{0:T(128)S(6)} %copy.13.nest_x_in, s32[1]{0:T(128)S(6)} %copy.14.nest_y_in, f32[5,1800,128]{2,1,0:T(8,128)} %bitcast.11, s32[36,1,128]{2,1,0:T(1,128)} %bitcast.14, f32[36,1,128]{2,1,0:T(1,128)} %bitcast.16, f32[12,384]{1,0:T(8,128)} %nudge_in.1, ...), custom_call_target="tpu_custom_call" | custom-call | tf_op jit(solution)/shard_map/exchange/pallas_call | solution.py:517
  30.8 9.3 %scatter.1 = f32[9000,128]{1,0:T(8,128)} custom-call(f32[64,128]{1,0:T(8,128)} %get-tuple-element.7.vals_in, s32[16,128]{1,0:T(8,128)} %bitcast.18, s32[1,128]{1,0:T(1,128)} %bitcast.19, f32[9000,128]{1,0:T(8,128)} %bitcast.12, s32[36,1,128]{2,1,0:T(1,128)} %bitcast.15), custom_call_target="tpu_custom_call" | custom-call | tf_op jit(solution)/shard_map/scatter/pallas_call | solution.py:532

commit v7 on v5

--- a/solution.py
+++ b/solution.py
@@ -489,7 +489,7 @@
         pltpu.VMEM((NF, NL, 1, NL), F32),
         pltpu.VMEM((SLOTS, 128), F32),
         pltpu.VMEM((NZA * 8, 128), F32),
-        pltpu.VMEM((NF, ROWS, 128), F32),
+        pltpu.VMEM((NF + 1, ROWS, 128), F32),
         pltpu.VMEM((NF, NXC + 2, NB, LP, 128), F32),
         pltpu.VMEM((NXC // 2, 192, 2 * NYC), BF16),
         pltpu.VMEM((NF, 64, 192), BF16),
@@ -507,7 +507,7 @@
         pltpu.VMEM((128, 128), F32),
         pltpu.VMEM((NTY, NTX, 128), F32),
         pltpu.VMEM((NTX, 128), F32),
-        pltpu.VMEM((NTX, 128), F32),
+        pltpu.VMEM((2 * NTX, 128), F32),
         pltpu.VMEM((NZA, 8, 128), F32),
         pltpu.VMEM((NZA, 8, 128), F32),
         DMA((NF,)), DMA((2, NF)), DMA((2, NF)), DMA((2,)), DMA((2,)), DMA((NF,)), DMA((NF,)),

time: 39.6 us -> 39.6 us (level)
  no operation moved by 1% of the time
where the time goes in v7:
time: 39.6 us; the launch traced here: 39.4 us
  Pallas kernels  38.1 us (96%)
  between operations  1.3 us (3%)
    pallas_call x1, Pallas kernels, local(): pl.pallas_call(exchange_kernel, out_shape=(jax.ShapeDtypeStruct((NF, ROWS...  28.9 us
    pallas_call x1, Pallas kernels, local(): pl.pallas_call(scatter_kernel, out_shape=jax.ShapeDtypeStruct((total, 128...  9.26 us

profile of v7, /device:TPU:25, one launch (start us, length us, event | category | flops | bytes accessed | tf_op | source)
XLA Modules:
  0.0 39.4 jit_solution(12076367427690722367)
XLA Ops:
  1.3 28.9 %exchange.1 = (f32[5,1800,128]{2,1,0:T(8,128)}, f32[64,128]{1,0:T(8,128)}) custom-call(s32[1]{0:T(128)S(6)} %copy.13.nest_x_in, s32[1]{0:T(128)S(6)} %copy.14.nest_y_in, f32[5,1800,128]{2,1,0:T(8,128)} %bitcast.11, s32[36,1,128]{2,1,0:T(1,128)} %bitcast.14, f32[36,1,128]{2,1,0:T(1,128)} %bitcast.16, f32[12,384]{1,0:T(8,128)} %nudge_in.1, ...), custom_call_target="tpu_custom_call" | custom-call | tf_op jit(solution)/shard_map/exchange/pallas_call | solution.py:517
  30.2 9.3 %scatter.1 = f32[9000,128]{1,0:T(8,128)} custom-call(f32[64,128]{1,0:T(8,128)} %get-tuple-element.7.vals_in, s32[16,128]{1,0:T(8,128)} %bitcast.18, s32[1,128]{1,0:T(1,128)} %bitcast.19, f32[9000,128]{1,0:T(8,128)} %bitcast.12, s32[36,1,128]{2,1,0:T(1,128)} %bitcast.15), custom_call_target="tpu_custom_call" | custom-call | tf_op jit(solution)/shard_map/scatter/pallas_call | solution.py:532
